TPU v7x, 512 devices: a whole 4x4x16 slice. The times are simulated.
512 devices in a mesh: row: 32 (over x, z_lo), col: 16 (over z_hi, y, core).
Axes of the slice: x: 4, y: 4, z: 16 (z_hi: 2, z_lo: 8; z = z_hi * 8 + z_lo), core: 2. Of those that a mesh axis runs over, the one named last changes fastest.
Arguments:
- amplitudes: float32 [3072, 4, 2048], P(('row', 'col')), may hold values from -6 to 6
- integrals: float32 [8192, 4, 2048], P('row', None, 'col'), may hold values from -0.0625 to 0.0625
Outputs:
- ladder: float32 [3072, 8192], P('col', 'row')
All inputs are finite; a program needn't handle non-finite values.
Results may differ from a plain program's by a relative error of at most 0.0001.
Values sent between devices are 32-bit elements; how exact they have to be, the bound alone decides.
No kernel may reach another device: no remote copies, remote signals or barrier semaphores. Data moves between devices by JAX's collectives and lax.ppermute only.
A program may use at most 64 MiB of HBM per device.

v0:
```python
import jax
import jax.numpy as jnp
from jax import lax
from jax.sharding import PartitionSpec as P

PANELS = 4


def contract(rows, weights):
    return lax.dot_general(
        rows,
        weights,
        (((1,), (1,)), ((), ())),
        precision=lax.Precision.HIGHEST,
        preferred_element_type=jnp.float32,
    )


def per_device(amplitudes, integrals):
    n_row = lax.axis_size("row")
    n_col = lax.axis_size("col")
    local_rows = amplitudes.shape[0]
    width = integrals.shape[2]
    all_rows = local_rows * n_row * n_col
    total = jnp.zeros((all_rows, integrals.shape[0]), jnp.float32)
    for panel in range(PANELS):
        piece = amplitudes[:, panel, :]
        weights = integrals[:, panel, :]
        spread = lax.all_gather(piece, "row", axis=0, tiled=True)
        mixed = lax.all_to_all(spread, "col", split_axis=1, concat_axis=0, tiled=True)
        ordered = (
            mixed.reshape(n_col, n_row, local_rows, width)
            .transpose(1, 0, 2, 3)
            .reshape(all_rows, width)
        )
        total = total + contract(ordered, weights)
    return lax.psum_scatter(total, "col", scatter_dimension=0, tiled=True)


def solution(mesh):
    in_specs = (P(("row", "col"), None, None), P("row", None, "col"))
    out_specs = P("col", "row")
    return jax.shard_map(
        per_device, mesh=mesh, in_specs=in_specs, out_specs=out_specs, check_vma=False
    )
```

profile of v0, /device:TPU:4, one launch (start us, length us, event | category | flops | bytes accessed | tf_op | source)
XLA Modules:
  0.0 1254.1 jit_solution(16290584040939222164)
XLA Ops:
  6.5 0.0 all-gather.9.cloned.1.call-start
  6.5 2.1 fusion.1
  8.6 0.0 all-gather.9.cloned.1.call-update
  8.6 211.9 %all-gather.9.cloned.1.call-done = f32[192,1,2048]{2,1,0:T(1,128)} async-done(((f32[6,1,2048]{2,1,0:T(1,128)}), f32[192,1,2048]{2,1,0:T(1,128)}) %all-gather.9.cloned.1.call-update) | async-done | bytes 1572880 | tf_op jit(solution)/shard_map/all_gather | solution.py:29
  220.5 3.1 copy.7
  223.5 14.9 %all-to-all-start = ((f32[192,16,128]{2,0,1:T(8,128)}), f32[192,16,128]{2,0,1:T(8,128)S(1)}, u32[]{:S(2)}, u32[]{:S(2)}) async-start(f32[192,16,128]{2,0,1:T(8,128)} %copy.7), calls=%async_computation | async-start | bytes 3145728 | tf_op jit(solution)/shard_map/all_to_all | solution.py:30
  238.5 0.0 all-gather.11.cloned.1.call-start
  238.5 0.7 all-gather.11.cloned.1.call-update
  239.2 243.2 %all-gather.11.cloned.1.call-done = f32[192,1,2048]{2,1,0:T(1,128)} async-done(((f32[6,1,2048]{2,1,0:T(1,128)}), f32[192,1,2048]{2,1,0:T(1,128)}) %all-gather.11.cloned.1.call-update) | async-done | bytes 1572880 | tf_op jit(solution)/shard_map/all_gather | solution.py:29
  482.4 3.1 copy.10
  485.5 0.0 all-to-all-done
  485.5 11.3 all-to-all-start.1
  496.8 0.0 all-gather.13.cloned.1.call-start
  496.9 0.7 all-gather.13.cloned.1.call-update
  497.6 241.2 %all-gather.13.cloned.1.call-done = f32[192,1,2048]{2,1,0:T(1,128)} async-done(((f32[6,1,2048]{2,1,0:T(1,128)}), f32[192,1,2048]{2,1,0:T(1,128)}) %all-gather.13.cloned.1.call-update) | async-done | bytes 1572880 | tf_op jit(solution)/shard_map/all_gather | solution.py:29
  738.8 3.1 copy.13
  741.9 0.0 all-to-all-done.1
  741.9 0.0 copy-start
  741.9 1.2 copy-done
  743.1 8.4 all-to-all-start.2
  751.5 0.0 all-gather.15.cloned.1.call-start
  751.5 0.5 all-gather.15.cloned.1.call-update
  752.0 246.9 %all-gather.15.cloned.1.call-done = f32[192,1,2048]{2,1,0:T(1,128)} async-done(((f32[6,1,2048]{2,1,0:T(1,128)}), f32[192,1,2048]{2,1,0:T(1,128)}) %all-gather.15.cloned.1.call-update) | async-done | bytes 1572880 | tf_op jit(solution)/shard_map/all_gather | solution.py:29
  999.0 3.1 copy.16
  1002.0 0.0 copy-start.4
  1002.0 0.0 all-to-all-done.2
  1002.0 13.9 %all-to-all-start.3 = ((f32[192,16,128]{2,0,1:T(8,128)}), f32[192,16,128]{2,0,1:T(8,128)}, u32[]{:S(2)}, u32[]{:S(2)}) async-start(f32[192,16,128]{2,0,1:T(8,128)} %copy.16), calls=%async_computation.3 | async-start | bytes 3145728 | tf_op jit(solution)/shard_map/all_to_all | solution.py:30
  1016.0 0.2 reduce-scatter.2.cloned.1.call-start
  1016.2 0.0 copy-done.4
  1016.2 0.4 fusion
  1016.6 0.9 copy.8
  1017.5 0.6 copy.9
  1018.1 1.4 reshape.41
  1019.5 2.3 copy.11
  1021.8 0.6 copy.12
  1022.4 1.4 reshape.43
  1023.8 2.3 copy.14
  1026.1 0.6 copy.15
  1026.8 1.4 reshape.45
  1028.1 59.8 %all-to-all-done.3 = f32[192,16,128]{2,0,1:T(8,128)} async-done(((f32[192,16,128]{2,0,1:T(8,128)}), f32[192,16,128]{2,0,1:T(8,128)}, u32[]{:S(2)}, u32[]{:S(2)}) %all-to-all-start.3) | async-done | bytes 1572896 | tf_op jit(solution)/shard_map/all_to_all | solution.py:30
  1087.9 2.3 copy.17
  1090.2 0.6 copy.18
  1090.9 1.3 reshape.47
  1092.2 0.0 copy-start.1
  1092.2 4.2 fusion.2
  1096.4 0.0 copy-done.1
  1096.4 0.0 copy-start.2
  1096.4 2.9 convolution_add_fusion.2
  1099.4 0.0 copy-done.2
  1099.4 0.0 copy-start.3
  1099.4 2.7 convolution_add_fusion.1
  1102.1 0.0 copy-done.3
  1102.1 4.3 convolution_add_fusion
  1106.4 0.0 reduce-scatter.2.cloned.1.call-update
  1106.4 141.1 %reduce-scatter.2.cloned.1.call-done = f32[192,256]{1,0:T(8,128)} async-done(((f32[3072,256]{1,0:T(8,128)}), f32[192,256]{1,0:T(8,128)}) %reduce-scatter.2.cloned.1.call-update) | async-done | bytes 196624 | tf_op jit(solution)/shard_map/reduce_scatter | solution.py:37
Async XLA Ops:
  6.5 213.9 %all-gather.9.cloned.1.call-start = ((), (), s32[]{:S(2)}) async-start(), calls=%async_computation.6 | async-start | bytes 1622016 | tf_op jit(solution)/shard_map/all_gather | solution.py:29
  223.5 262.0 %all-to-all-start = ((f32[192,16,128]{2,0,1:T(8,128)}), f32[192,16,128]{2,0,1:T(8,128)S(1)}, u32[]{:S(2)}, u32[]{:S(2)}) async-start(f32[192,16,128]{2,0,1:T(8,128)} %copy.7), calls=%async_computation | async-start | bytes 3145728 | tf_op jit(solution)/shard_map/all_to_all | solution.py:30
  238.5 243.9 %all-gather.11.cloned.1.call-start = ((), (), s32[]{:S(2)}) async-start(), calls=%async_computation.7 | async-start | bytes 1622016 | tf_op jit(solution)/shard_map/all_gather | solution.py:29
  485.5 256.3 %all-to-all-start.1 = ((f32[192,16,128]{2,0,1:T(8,128)}), f32[192,16,128]{2,0,1:T(8,128)S(1)}, u32[]{:S(2)}, u32[]{:S(2)}) async-start(f32[192,16,128]{2,0,1:T(8,128)} %copy.10), calls=%async_computation.1 | async-start | bytes 3145728 | tf_op jit(solution)/shard_map/all_to_all | solution.py:30
  496.8 241.9 %all-gather.13.cloned.1.call-start = ((), (), s32[]{:S(2)}) async-start(), calls=%async_computation.8 | async-start | bytes 1622016 | tf_op jit(solution)/shard_map/all_gather | solution.py:29
  741.9 1.2 copy-start
  743.1 259.0 %all-to-all-start.2 = ((f32[192,16,128]{2,0,1:T(8,128)}), f32[192,16,128]{2,0,1:T(8,128)}, u32[]{:S(2)}, u32[]{:S(2)}) async-start(f32[192,16,128]{2,0,1:T(8,128)} %copy.13), calls=%async_computation.2 | async-start | bytes 3145728 | tf_op jit(solution)/shard_map/all_to_all | solution.py:30
  751.5 247.5 %all-gather.15.cloned.1.call-start = ((), (), s32[]{:S(2)}) async-start(), calls=%async_computation.9 | async-start | bytes 1622016 | tf_op jit(solution)/shard_map/all_gather | solution.py:29
  1002.0 14.2 %copy-start.4 = (f32[256,4,128]{2,1,0:T(4,128)S(1)}, f32[256,4,128]{2,1,0:T(4,128)}, u32[]{:S(2)}) copy-start(f32[256,4,128]{2,1,0:T(4,128)} %param.3) | copy-start | bytes 1572868
  1002.0 85.9 %all-to-all-start.3 = ((f32[192,16,128]{2,0,1:T(8,128)}), f32[192,16,128]{2,0,1:T(8,128)}, u32[]{:S(2)}, u32[]{:S(2)}) async-start(f32[192,16,128]{2,0,1:T(8,128)} %copy.16), calls=%async_computation.3 | async-start | bytes 3145728 | tf_op jit(solution)/shard_map/all_to_all | solution.py:30
  1016.0 231.6 %reduce-scatter.2.cloned.1.call-start = ((), (), s32[]{:S(2)}) async-start(), calls=%async_computation.5 | async-start | bytes 3342336 | tf_op jit(solution)/shard_map/reduce_scatter | solution.py:37
  1092.2 4.2 copy-start.1
  1096.4 3.0 copy-start.2
  1099.4 2.7 copy-start.3
Sparse Core Ops, SparseCore 0:
  9.4 211.0 all-gather.8
  241.4 241.0 all-gather.10
  499.7 239.0 all-gather.12
  754.0 244.8 all-gather.14
  1106.6 140.9 reduce-scatter.1
where the time goes:
time: 1250 us
  waiting for transfers between devices  1150 us (92%)
  starting transfers between devices  48.9 us (4%)
  local copies, waits for them, and re-layouts  31.7 us (3%)
  matrix products  14.1 us (1%)
  between operations  13.3 us (1%)
    all_gather x4, waiting for transfers between devices, per_device(): spread = lax.all_gather(piece, 'row', axis=0, tiled=True)  943 us
    reduce_scatter x1, waiting for transfers between devices, per_device(): return lax.psum_scatter(total, 'col', scatter_dimension=0, tiled=True)  141 us
    all_to_all x4, waiting for transfers between devices, per_device(): lax.all_to_all(spread, 'col', split_axis=1, concat_axis=0, tiled=True)  59.8 us
    all_to_all x4, starting transfers between devices, per_device(): lax.all_to_all(spread, 'col', split_axis=1, concat_axis=0, tiled=True)  48.5 us
  transfers between devices with their start and end apart: 9, of which 6 were waited for; matrix products, arithmetic and copies ran while one was open for 2% of the time, Pallas kernels for 0%

commit v1 on v0

v1 whole, which is shorter than its diff:
```python
import jax
import jax.numpy as jnp
from jax import lax
from jax.sharding import PartitionSpec as P


def per_device(amplitudes, integrals):
    width = integrals.shape[2]
    depth = amplitudes.shape[1] * width
    mixed = lax.all_to_all(amplitudes, "col", split_axis=2, concat_axis=0, tiled=True)
    mixed = mixed.reshape(mixed.shape[0], depth)
    weights = integrals.reshape(integrals.shape[0], depth)
    rows = lax.all_gather(mixed, "row", axis=0, tiled=True)
    total = lax.dot_general(
        rows,
        weights,
        (((1,), (1,)), ((), ())),
        precision=lax.Precision.HIGH,
        preferred_element_type=jnp.float32,
    )
    return lax.psum_scatter(total, "col", scatter_dimension=0, tiled=True)


def solution(mesh):
    in_specs = (P(("row", "col"), None, None), P("row", None, "col"))
    out_specs = P("col", "row")
    return jax.shard_map(
        per_device, mesh=mesh, in_specs=in_specs, out_specs=out_specs, check_vma=False
    )
```

time: 1250 us -> 456 us (0.36)
  waiting for transfers between devices: 1150 us -> 378 us
  starting transfers between devices: 48.9 us -> 0.04 us
  blocking collectives: 0 us -> 34 us
    all_gather x4 -> x1, waiting for transfers between devices: 943 us -> 225 us  [per_device(): rows = lax.all_gather(mixed, 'row', axis=0, tiled=True)]
    all_to_all x4 -> x0, waiting for transfers between devices: 59.8 us -> none  [per_device(): lax.all_to_all(spread, 'col', split_axis=1, concat_axis=0, tiled=True)]
    all_to_all x4 -> x0, starting transfers between devices: 48.5 us -> none  [per_device(): lax.all_to_all(spread, 'col', split_axis=1, concat_axis=0, tiled=True)]
    all_to_all x0 -> x1, blocking collectives: none -> 34 us  [per_device(): lax.all_to_all(amplitudes, 'col', split_axis=2, concat_axis=0, tiled=True)]
    unnamed x10 -> x6, local copies, waits for them, and re-layouts: 1.22 us -> 18.4 us
    all_to_all x8 -> x2, local copies, waits for them, and re-layouts: 20.2 us -> 4.04 us  [per_device(): lax.all_to_all(amplitudes, 'col', split_axis=2, concat_axis=0, tiled=True)]
  transfers between devices with their start and end apart: 9 -> 2, of which waited for: 6 -> 2; matrix products, arithmetic and copies ran while one was open for 2% -> 0% of each run, Pallas kernels for 0% -> 0%
where the time goes in v1:
time: 456 us
  waiting for transfers between devices  378 us (83%)
  blocking collectives  34 us (7%)
  local copies, waits for them, and re-layouts  22.4 us (5%)
  between operations  13.4 us (3%)
  matrix products  7.13 us (2%)
    all_gather x1, waiting for transfers between devices, per_device(): rows = lax.all_gather(mixed, 'row', axis=0, tiled=True)  225 us
    reduce_scatter x1, waiting for transfers between devices, per_device(): return lax.psum_scatter(total, 'col', scatter_dimension=0, tiled=True)  153 us
    all_to_all x1, blocking collectives, per_device(): lax.all_to_all(amplitudes, 'col', split_axis=2, concat_axis=0, tiled=True)  34 us
    unnamed x6, local copies, waits for them, and re-layouts  18.4 us
  transfers between devices with their start and end apart: 2, of which 2 were waited for; matrix products, arithmetic and copies ran while one was open for 0% of the time, Pallas kernels for 0%

profile of v1, /device:TPU:4, one launch (start us, length us, event | category | flops | bytes accessed | tf_op | source)
XLA Modules:
  0.0 456.0 jit_solution(1031899282822324098)
XLA Ops:
  6.5 0.0 all-gather.2.cloned.1.call-start
  6.5 4.3 copy.6
  10.8 0.0 copy-start
  10.8 6.6 %reshape.9 = f32[16,1,3072]{2,1,0:T(1,128)S(1)} reshape(f32[2048,4,6]{2,1,0:T(4,128)} %bitcast.15) | data formatting | bytes 393216
  17.4 34.0 %all_to_all.15 = f32[16,1,3072]{2,1,0:T(1,128)S(1)} all-to-all(f32[16,1,3072]{2,1,0:T(1,128)S(1)} %reshape.9), channel_id=1, replica_groups=mesh['row'=32,'col'=16] {'col'}, dimensions={0} | all-to-all | bytes 393216 | tf_op jit(solution)/shard_map/all_to_all | solution.py:10
  51.4 0.5 broadcast
  51.9 1.1 reduce
  53.0 6.8 %reshape.10 = f32[2048,4,6]{2,1,0:T(4,128)} reshape(f32[16,3072]{1,0:T(8,128)S(1)} %reduce) | data formatting | bytes 393216
  59.8 3.5 copy.7
  63.3 0.7 copy.15
  64.0 0.0 all-gather.2.cloned.1.call-update
  64.1 0.0 reduce-scatter.2.cloned.1.call-start
  64.1 224.6 %all-gather.2.cloned.1.call-done = f32[3072,512]{1,0:T(8,128)} async-done(((f32[96,512]{1,0:T(8,128)}), f32[3072,512]{1,0:T(8,128)}) %all-gather.2.cloned.1.call-update) | async-done | bytes 6291472 | tf_op jit(solution)/shard_map/all_gather | solution.py:13
  288.7 0.0 copy-done
  288.7 7.1 %fusion = f32[3072,256]{1,0:T(8,128)} fusion(f32[3072,512]{1,0:T(8,128)} %all-gather.2.cloned.1.call-done, f32[32,8,4,128]{3,2,1,0:T(4,128)S(1)} %bitcast.18), kind=kOutput, calls=%fused_computation | convolution fusion | flops 2415919104 | bytes 9961472 | tf_op jit(solution)/shard_map/dot_general | solution.py:14
  295.9 0.0 reduce-scatter.2.cloned.1.call-update
  295.9 153.2 %reduce-scatter.2.cloned.1.call-done = f32[192,256]{1,0:T(8,128)} async-done(((f32[3072,256]{1,0:T(8,128)}), f32[192,256]{1,0:T(8,128)}) %reduce-scatter.2.cloned.1.call-update) | async-done | bytes 196624 | tf_op jit(solution)/shard_map/reduce_scatter | solution.py:21
Async XLA Ops:
  6.5 282.2 %all-gather.2.cloned.1.call-start = ((), (), s32[]{:S(2)}) async-start(), calls=%async_computation.2 | async-start | bytes 6488064 | tf_op jit(solution)/shard_map/all_gather | solution.py:13
  10.8 277.9 %copy-start = (f32[256,4,128]{2,1,0:T(4,128)S(1)}, f32[256,4,128]{2,1,0:T(4,128)}, u32[]{:S(2)}) copy-start(f32[256,4,128]{2,1,0:T(4,128)} %param.3) | copy-start | bytes 1572868
  64.1 385.1 %reduce-scatter.2.cloned.1.call-start = ((), (), s32[]{:S(2)}) async-start(), calls=%async_computation.3 | async-start | bytes 3342336 | tf_op jit(solution)/shard_map/reduce_scatter | solution.py:21
Sparse Core Ops, SparseCore 0:
  64.2 224.4 all-gather.1
  296.0 153.0 reduce-scatter.1

commit v2 on v1

v2 whole, which is shorter than its diff:
```python
import jax
import jax.numpy as jnp
from jax import lax
from jax.sharding import Mesh
from jax.sharding import PartitionSpec as P

AXES = ("x", "s", "p", "zh", "y", "c")
SIZES = (4, 4, 2, 2, 4, 2)


def split(value):
    high = lax.reduce_precision(value, 8, 7)
    return high.astype(jnp.bfloat16), (value - high).astype(jnp.bfloat16)


def contract(rows, weights):
    return lax.dot_general(
        rows, weights, (((1,), (1,)), ((), ())), preferred_element_type=jnp.float32
    )


def shift(value, axis, by):
    size = lax.axis_size(axis)
    return lax.ppermute(value, axis, [((i + by) % size, i) for i in range(size)])


def rolled(value, by, axis):
    size = value.shape[axis]
    twice = jnp.concatenate([value, value], axis=axis)
    return lax.dynamic_slice_in_dim(twice, by, size, axis=axis)


def per_device(amplitudes, integrals):
    nx, ns, np_, nzh, ny, nc = SIZES
    rows, panels, _ = amplitudes.shape
    block, _, width = integrals.shape
    depth = panels * width
    x, p, c = (lax.axis_index(a) for a in ("x", "p", "c"))

    own = integrals.reshape(block, depth)
    pair = shift(own, "p", 1)
    weights = jnp.zeros((nx * np_, block, 3 * depth), jnp.bfloat16)
    for e, part in enumerate((own, pair)):
        for d in range(nx):
            piece = part
            if d:
                piece = shift(part, "x", d)
            place = np_ * ((x + d) % nx) + (p + e) % np_
            high, low = split(piece)
            piece = jnp.concatenate([high, low, high], axis=1)
            weights = lax.dynamic_update_slice_in_dim(weights, piece[None], place, 0)
    weights = weights.reshape(nx * np_ * block, 3 * depth)

    swap = [(a * ny + b, b * nx + a) for a in range(nx) for b in range(ny)]
    moved = lax.ppermute(amplitudes, ("x", "y"), swap)
    moved = moved.reshape(rows, panels, nzh, ny * nc, width).transpose(3, 2, 0, 1, 4)
    spread = lax.all_to_all(moved, ("y", "c"), 0, 0, tiled=True)
    spread = spread.transpose(1, 0, 2, 3, 4).reshape(nzh, 1, nx * nc * rows, depth)
    spread = jnp.broadcast_to(spread, (nzh, ns) + spread.shape[2:])
    spread = spread.reshape((nzh * ns,) + spread.shape[2:])
    held = lax.all_to_all(spread, ("zh", "s"), 0, 0, tiled=True)
    held = held.reshape(nzh, 2, 2, 2, 2, nc, rows, depth)
    held = held.transpose(2, 4, 1, 3, 0, 5, 6, 7)
    held = rolled(held, c, 0)
    group = nzh * nc * rows
    high, low = split(held.reshape(2, 8 * group, depth))
    held = jnp.concatenate([high, high, low], axis=2)

    away = contract(held[1], weights)
    home = contract(held[0], weights)
    home = home + shift(away, "c", 1)
    home = home.reshape(ny, 2 * group, home.shape[1])
    home = lax.all_to_all(home, "y", 0, 0, tiled=True)
    home = (home[0] + home[1]) + (home[2] + home[3])

    home = home.reshape(nzh, group, nx * np_, block).transpose(0, 2, 1, 3)
    home = home.reshape(nzh * nx * np_, group, block)
    out = lax.all_to_all(home, ("zh", "x", "p"), 0, 0, tiled=True)
    out = out.reshape(nzh, ny, np_, nzh, nc * rows, block)
    out = (out[0] + out[1]).transpose(1, 2, 0, 3, 4)
    return out.reshape(np_ * nzh * ny * nc * rows, block)


def solution(mesh):
    fine = Mesh(mesh.devices.reshape(SIZES), AXES)
    in_specs = (P(AXES, None, None), P(AXES[:3], None, AXES[3:]))
    out_specs = P(AXES[3:], AXES[:3])
    return jax.shard_map(
        per_device, mesh=fine, in_specs=in_specs, out_specs=out_specs, check_vma=False
    )
```

time: 456 us -> 192 us (0.42)
  the two profiles are of different devices: /device:TPU:4 before, /device:TPU:32 now
where the time goes in v2:
time: 192 us
  starting transfers between devices  67.9 us (35%)
  blocking collectives  61 us (32%)
  waiting for transfers between devices  28.9 us (15%)
  other arithmetic  12.2 us (6%)
  local copies, waits for them, and re-layouts  11.3 us (6%)
  matrix products  9.95 us (5%)
    all_to_all x1, blocking collectives, per_device(): out = lax.all_to_all(home, ('zh', 'x', 'p'), 0, 0, tiled=True)  37.3 us
    all_to_all x1, starting transfers between devices, per_device(): spread = lax.all_to_all(moved, ('y', 'c'), 0, 0, tiled=True)  25.9 us
    ppermute x8, starting transfers between devices, shift(): lax.ppermute(value, axis, [((i + by) % size, i) for i in range(size)])  24.9 us
    all_to_all x1, blocking collectives, per_device(): home = lax.all_to_all(home, 'y', 0, 0, tiled=True)  23.7 us
    ppermute x8, waiting for transfers between devices, shift(): lax.ppermute(value, axis, [((i + by) % size, i) for i in range(size)])  22.1 us
    all_to_all x1, starting transfers between devices, per_device(): held = lax.all_to_all(spread, ('zh', 's'), 0, 0, tiled=True)  14.2 us
    dot_general x2, matrix products, contract(): lax.dot_general(rows, weights, (((1,), (1,)), ((), ())), preferred_elemen...  9.95 us
    dynamic_update_slice x8, other arithmetic, per_device(): weights = lax.dynamic_update_slice_in_dim(weights, piece[None], place, 0)  7.66 us
  transfers between devices with their start and end apart: 11, of which 6 were waited for; matrix products, arithmetic and copies ran while one was open for 8% of the time, Pallas kernels for 0%

profile of v2, /device:TPU:32, one launch (start us, length us, event | category | flops | bytes accessed | tf_op | source)
XLA Modules:
  0.0 191.6 jit_solution(16192124060406976208)
XLA Ops:
  0.0 1.1 copy.44
  1.1 4.7 %collective-permute-start.1 = (f32[256,512]{1,0:T(8,128)S(1)}, f32[256,512]{1,0:T(8,128)S(1)}, u32[]{:S(2)}, u32[]{:S(2)}) collective-permute-start(f32[256,512]{1,0:T(8,128)S(1)} %bitcast.81), channel_id=1, source_target_pairs={{128,0},{256,128},{384,256},{0,384},{129,1},{257,129},{385,257},{1... | collective-permute-start | bytes 1572872 | tf_op jit(solution)/shard_map/ppermute | solution.py:24
  5.8 2.7 %collective-permute-start.2 = (f32[256,512]{1,0:T(8,128)S(1)}, f32[256,512]{1,0:T(8,128)S(1)}, u32[]{:S(2)}, u32[]{:S(2)}) collective-permute-start(f32[256,512]{1,0:T(8,128)S(1)} %bitcast.82), channel_id=1, source_target_pairs={{256,0},{384,128},{0,256},{128,384},{257,1},{385,129},{1,257},{129... | collective-permute-start | bytes 1572872 | tf_op jit(solution)/shard_map/ppermute | solution.py:24
  8.5 2.8 %collective-permute-start.3 = (f32[256,512]{1,0:T(8,128)S(1)}, f32[256,512]{1,0:T(8,128)S(1)}, u32[]{:S(2)}, u32[]{:S(2)}) collective-permute-start(f32[256,512]{1,0:T(8,128)S(1)} %bitcast.83), channel_id=1, source_target_pairs={{384,0},{0,128},{128,256},{256,384},{385,1},{1,129},{129,257},{257... | collective-permute-start | bytes 1572872 | tf_op jit(solution)/shard_map/ppermute | solution.py:24
  11.3 5.0 %collective-permute-start.4 = (f32[256,512]{1,0:T(8,128)S(1)}, f32[256,512]{1,0:T(8,128)S(1)}, u32[]{:S(2)}, u32[]{:S(2)}) collective-permute-start(f32[256,512]{1,0:T(8,128)S(1)} %bitcast.84), channel_id=1, source_target_pairs={{16,0},{0,16},{17,1},{1,17},{18,2},{2,18},{19,3},{3,19},{20,4},{4,... | collective-permute-start | bytes 1572872 | tf_op jit(solution)/shard_map/ppermute | solution.py:24
  16.2 3.0 %collective-permute-start = (f32[6,4,2048]{2,1,0:T(4,128)}, f32[6,4,2048]{2,1,0:T(4,128)}, u32[]{:S(2)}, u32[]{:S(2)}) collective-permute-start(f32[6,4,2048]{2,1,0:T(4,128)} %param.2), channel_id=1, source_target_pairs={{0,0},{2,128},{4,256},{6,384},{128,2},{130,130},{132,258},{134,386... | collective-permute-start | bytes 589832 | tf_op jit(solution)/shard_map/ppermute | solution.py:55
  19.2 1.1 fusion.15
  20.4 0.0 collective-permute-done
  20.4 1.0 reshape.43
  21.4 0.8 copy.20
  22.2 25.9 %all-to-all-start = ((f32[8,2,6,4,128]{4,3,2,1,0:T(4,128)}), f32[8,2,6,4,128]{4,3,2,1,0:T(4,128)S(1)}, u32[]{:S(2)}, u32[]{:S(2)}) async-start(f32[8,2,6,4,128]{4,3,2,1,0:T(4,128)} %copy.20), calls=%async_computation | async-start | bytes 393216 | tf_op jit(solution)/shard_map/all_to_all | solution.py:57
  48.0 3.2 %broadcast_in_dim.36 = bf16[8,256,1536]{2,1,0:T(8,128)(2,1)} broadcast(bf16[]{:T(256)} %constant.72.clone.1), dimensions={} | broadcast | bytes 6291458 | tf_op jit(solution)/shard_map/broadcast_in_dim | solution.py:42
  51.2 1.0 fusion.2
  52.2 2.6 %all-to-all-done = f32[8,2,6,4,128]{4,3,2,1,0:T(4,128)S(1)} async-done(((f32[8,2,6,4,128]{4,3,2,1,0:T(4,128)}), f32[8,2,6,4,128]{4,3,2,1,0:T(4,128)S(1)}, u32[]{:S(2)}, u32[]{:S(2)}) %all-to-all-start) | async-done | bytes 196640 | tf_op jit(solution)/shard_map/all_to_all | solution.py:57
  54.9 0.1 broadcast_in_dim.34
  54.9 1.0 broadcast_in_dim.35
  55.9 14.2 %all-to-all-start.1 = ((f32[8,48,512]{2,1,0:T(8,128)}), f32[8,48,512]{2,1,0:T(8,128)S(1)}, u32[]{:S(2)}, u32[]{:S(2)}) async-start(f32[8,48,512]{2,1,0:T(8,128)} %bitcast.2), calls=%async_computation.1 | async-start | bytes 1572864 | tf_op jit(solution)/shard_map/all_to_all | solution.py:61
  70.1 0.0 collective-permute-done.1
  70.1 0.1 fusion.16
  70.2 1.0 fusion.3
  71.2 0.0 collective-permute-done.4
  71.2 1.9 collective-permute-start.5
  73.1 0.0 collective-permute-done.2
  73.1 0.1 fusion.17
  73.2 0.9 fusion.4
  74.1 0.0 collective-permute-done.3
  74.1 0.1 fusion.18
  74.2 0.9 fusion.5
  75.2 2.8 %collective-permute-start.6 = (f32[256,512]{1,0:T(8,128)S(1)}, f32[256,512]{1,0:T(8,128)S(1)}, u32[]{:S(2)}, u32[]{:S(2)}) collective-permute-start(f32[256,512]{1,0:T(8,128)S(1)} %collective-permute-done.4), channel_id=1, source_target_pairs={{256,0},{384,128},{0,256},{128,384},{257,1},{385,129},{1,257},{129... | collective-permute-start | bytes 1572872 | tf_op jit(solution)/shard_map/ppermute | solution.py:24
  78.0 0.1 fusion.19
  78.0 1.0 fusion.6
  79.0 3.1 %collective-permute-start.7 = (f32[256,512]{1,0:T(8,128)S(1)}, f32[256,512]{1,0:T(8,128)S(1)}, u32[]{:S(2)}, u32[]{:S(2)}) collective-permute-start(f32[256,512]{1,0:T(8,128)S(1)} %collective-permute-done.4), channel_id=1, source_target_pairs={{384,0},{0,128},{128,256},{256,384},{385,1},{1,129},{129,257},{257... | collective-permute-start | bytes 1572872 | tf_op jit(solution)/shard_map/ppermute | solution.py:24
  82.1 5.7 %collective-permute-done.5 = f32[256,512]{1,0:T(8,128)S(1)} collective-permute-done((f32[256,512]{1,0:T(8,128)S(1)}, f32[256,512]{1,0:T(8,128)S(1)}, u32[]{:S(2)}, u32[]{:S(2)}) %collective-permute-start.5) | collective-permute-done | bytes 524320 | tf_op jit(solution)/shard_map/ppermute | solution.py:24
  87.9 0.1 fusion.20
  87.9 1.0 fusion.7
  88.9 4.5 %collective-permute-done.6 = f32[256,512]{1,0:T(8,128)S(1)} collective-permute-done((f32[256,512]{1,0:T(8,128)S(1)}, f32[256,512]{1,0:T(8,128)S(1)}, u32[]{:S(2)}, u32[]{:S(2)}) %collective-permute-start.6) | collective-permute-done | bytes 524320 | tf_op jit(solution)/shard_map/ppermute | solution.py:24
  93.4 0.1 fusion.21
  93.5 1.0 fusion.8
  94.4 8.5 %collective-permute-done.7 = f32[256,512]{1,0:T(8,128)S(1)} collective-permute-done((f32[256,512]{1,0:T(8,128)S(1)}, f32[256,512]{1,0:T(8,128)S(1)}, u32[]{:S(2)}, u32[]{:S(2)}) %collective-permute-start.7) | collective-permute-done | bytes 524320 | tf_op jit(solution)/shard_map/ppermute | solution.py:24
  102.9 0.1 fusion.22
  103.0 1.0 fusion.9
  103.9 4.2 %all-to-all-done.1 = f32[8,48,512]{2,1,0:T(8,128)S(1)} async-done(((f32[8,48,512]{2,1,0:T(8,128)}), f32[8,48,512]{2,1,0:T(8,128)S(1)}, u32[]{:S(2)}, u32[]{:S(2)}) %all-to-all-start.1) | async-done | bytes 786464 | tf_op jit(solution)/shard_map/all_to_all | solution.py:61
  108.1 0.5 copy.22
  108.6 0.5 reshape.45
  109.1 1.1 fusion.1
  110.2 0.4 copy.23
  110.6 0.5 reduce-precision_convert_fusion
  111.1 1.1 pad_maximum_fusion
  112.3 1.6 fusion.24
  113.9 5.0 %fusion.10 = f32[192,2048]{1,0:T(8,128)S(1)} fusion(bf16[2048,1536]{1,0:T(8,128)(2,1)} %bitcast.13, bf16[1,192,1536]{2,0,1:T(2,128)(2,1)S(1)} %get-tuple-element.6), kind=kOutput, calls=%fused_computation.40 | convolution fusion | flops 1207959552 | bytes 8454144 | tf_op jit(solution)/shard_map/dot_general | solution.py:17
  118.9 1.9 %collective-permute-start.8 = (f32[192,2048]{1,0:T(8,128)S(1)}, f32[192,2048]{1,0:T(8,128)S(1)}, u32[]{:S(2)}, u32[]{:S(2)}) collective-permute-start(f32[192,2048]{1,0:T(8,128)S(1)} %fusion.10), channel_id=1, source_target_pairs={{1,0},{0,1},{3,2},{2,3},{5,4},{4,5},{7,6},{6,7},{9,8},{8,9},{11,10... | collective-permute-start | bytes 4718600 | tf_op jit(solution)/shard_map/ppermute | solution.py:24
  120.8 3.4 %collective-permute-done.8 = f32[192,2048]{1,0:T(8,128)S(1)} collective-permute-done((f32[192,2048]{1,0:T(8,128)S(1)}, f32[192,2048]{1,0:T(8,128)S(1)}, u32[]{:S(2)}, u32[]{:S(2)}) %collective-permute-start.8) | collective-permute-done | bytes 1572896 | tf_op jit(solution)/shard_map/ppermute | solution.py:24
  124.2 5.0 %convolution_add_fusion = f32[192,2048]{1,0:T(8,128)S(1)} fusion(f32[192,2048]{1,0:T(8,128)S(1)} %collective-permute-done.8, bf16[2048,1536]{1,0:T(8,128)(2,1)} %bitcast.13, bf16[1,192,1536]{2,0,1:T(2,128)(2,1)S(1)} %get-tuple-element.5), kind=kOutput, calls=%fused_computation | convolution fusion | flops 1208352768 | bytes 10027008 | tf_op jit(solution)/shard_map/dot_general | solution.py:17
  129.2 23.7 %all_to_all.20 = f32[4,48,2048]{2,1,0:T(8,128)S(1)} all-to-all(f32[4,48,2048]{2,1,0:T(8,128)S(1)} %bitcast.71), channel_id=1, replica_groups=mesh['x'=4,'s'=4,'p'=2,'zh'=2,'y'=4,'c'=2] {'y'}, dimensions={0} | all-to-all | bytes 3145728 | tf_op jit(solution)/shard_map/all_to_all | solution.py:73
  152.9 0.1 fusion.23
  153.0 0.1 copy.30
  153.2 0.1 copy.24
  153.3 37.3 %all_to_all.21 = f32[16,24,256]{2,1,0:T(8,128)S(1)} all-to-all(f32[16,24,256]{2,1,0:T(8,128)S(1)} %bitcast.76), channel_id=1, replica_groups=mesh['x'=4,'s'=4,'p'=2,'zh'=2,'y'=4,'c'=2] {'zh','x','p'}, dimensions={0} | all-to-all | bytes 786432 | tf_op jit(solution)/shard_map/all_to_all | solution.py:78
  190.6 0.1 copy.25
  190.7 0.1 add.157
  190.8 0.1 copy.26
  190.9 0.7 reshape.51
  (3 shorter events, 0.1 us)
Async XLA Ops:
  1.1 69.1 %collective-permute-start.1 = (f32[256,512]{1,0:T(8,128)S(1)}, f32[256,512]{1,0:T(8,128)S(1)}, u32[]{:S(2)}, u32[]{:S(2)}) collective-permute-start(f32[256,512]{1,0:T(8,128)S(1)} %bitcast.81), channel_id=1, source_target_pairs={{128,0},{256,128},{384,256},{0,384},{129,1},{257,129},{385,257},{1... | collective-permute-start | bytes 1572872 | tf_op jit(solution)/shard_map/ppermute | solution.py:24
  5.8 67.4 %collective-permute-start.2 = (f32[256,512]{1,0:T(8,128)S(1)}, f32[256,512]{1,0:T(8,128)S(1)}, u32[]{:S(2)}, u32[]{:S(2)}) collective-permute-start(f32[256,512]{1,0:T(8,128)S(1)} %bitcast.82), channel_id=1, source_target_pairs={{256,0},{384,128},{0,256},{128,384},{257,1},{385,129},{1,257},{129... | collective-permute-start | bytes 1572872 | tf_op jit(solution)/shard_map/ppermute | solution.py:24
  8.5 65.7 %collective-permute-start.3 = (f32[256,512]{1,0:T(8,128)S(1)}, f32[256,512]{1,0:T(8,128)S(1)}, u32[]{:S(2)}, u32[]{:S(2)}) collective-permute-start(f32[256,512]{1,0:T(8,128)S(1)} %bitcast.83), channel_id=1, source_target_pairs={{384,0},{0,128},{128,256},{256,384},{385,1},{1,129},{129,257},{257... | collective-permute-start | bytes 1572872 | tf_op jit(solution)/shard_map/ppermute | solution.py:24
  11.3 59.9 %collective-permute-start.4 = (f32[256,512]{1,0:T(8,128)S(1)}, f32[256,512]{1,0:T(8,128)S(1)}, u32[]{:S(2)}, u32[]{:S(2)}) collective-permute-start(f32[256,512]{1,0:T(8,128)S(1)} %bitcast.84), channel_id=1, source_target_pairs={{16,0},{0,16},{17,1},{1,17},{18,2},{2,18},{19,3},{3,19},{20,4},{4,... | collective-permute-start | bytes 1572872 | tf_op jit(solution)/shard_map/ppermute | solution.py:24
  16.2 4.1 %collective-permute-start = (f32[6,4,2048]{2,1,0:T(4,128)}, f32[6,4,2048]{2,1,0:T(4,128)}, u32[]{:S(2)}, u32[]{:S(2)}) collective-permute-start(f32[6,4,2048]{2,1,0:T(4,128)} %param.2), channel_id=1, source_target_pairs={{0,0},{2,128},{4,256},{6,384},{128,2},{130,130},{132,258},{134,386... | collective-permute-start | bytes 589832 | tf_op jit(solution)/shard_map/ppermute | solution.py:55
  22.2 32.7 %all-to-all-start = ((f32[8,2,6,4,128]{4,3,2,1,0:T(4,128)}), f32[8,2,6,4,128]{4,3,2,1,0:T(4,128)S(1)}, u32[]{:S(2)}, u32[]{:S(2)}) async-start(f32[8,2,6,4,128]{4,3,2,1,0:T(4,128)} %copy.20), calls=%async_computation | async-start | bytes 393216 | tf_op jit(solution)/shard_map/all_to_all | solution.py:57
  55.9 52.2 %all-to-all-start.1 = ((f32[8,48,512]{2,1,0:T(8,128)}), f32[8,48,512]{2,1,0:T(8,128)S(1)}, u32[]{:S(2)}, u32[]{:S(2)}) async-start(f32[8,48,512]{2,1,0:T(8,128)} %bitcast.2), calls=%async_computation.1 | async-start | bytes 1572864 | tf_op jit(solution)/shard_map/all_to_all | solution.py:61
  71.2 16.7 %collective-permute-start.5 = (f32[256,512]{1,0:T(8,128)S(1)}, f32[256,512]{1,0:T(8,128)S(1)}, u32[]{:S(2)}, u32[]{:S(2)}) collective-permute-start(f32[256,512]{1,0:T(8,128)S(1)} %collective-permute-done.4), channel_id=1, source_target_pairs={{128,0},{256,128},{384,256},{0,384},{129,1},{257,129},{385,257},{1... | collective-permute-start | bytes 1572872 | tf_op jit(solution)/shard_map/ppermute | solution.py:24
  75.2 18.2 %collective-permute-start.6 = (f32[256,512]{1,0:T(8,128)S(1)}, f32[256,512]{1,0:T(8,128)S(1)}, u32[]{:S(2)}, u32[]{:S(2)}) collective-permute-start(f32[256,512]{1,0:T(8,128)S(1)} %collective-permute-done.4), channel_id=1, source_target_pairs={{256,0},{384,128},{0,256},{128,384},{257,1},{385,129},{1,257},{129... | collective-permute-start | bytes 1572872 | tf_op jit(solution)/shard_map/ppermute | solution.py:24
  79.0 23.9 %collective-permute-start.7 = (f32[256,512]{1,0:T(8,128)S(1)}, f32[256,512]{1,0:T(8,128)S(1)}, u32[]{:S(2)}, u32[]{:S(2)}) collective-permute-start(f32[256,512]{1,0:T(8,128)S(1)} %collective-permute-done.4), channel_id=1, source_target_pairs={{384,0},{0,128},{128,256},{256,384},{385,1},{1,129},{129,257},{257... | collective-permute-start | bytes 1572872 | tf_op jit(solution)/shard_map/ppermute | solution.py:24
  118.9 5.3 %collective-permute-start.8 = (f32[192,2048]{1,0:T(8,128)S(1)}, f32[192,2048]{1,0:T(8,128)S(1)}, u32[]{:S(2)}, u32[]{:S(2)}) collective-permute-start(f32[192,2048]{1,0:T(8,128)S(1)} %fusion.10), channel_id=1, source_target_pairs={{1,0},{0,1},{3,2},{2,3},{5,4},{4,5},{7,6},{6,7},{9,8},{8,9},{11,10... | collective-permute-start | bytes 4718600 | tf_op jit(solution)/shard_map/ppermute | solution.py:24

commit v3 on v2

v3 whole, which is shorter than its diff:
```python
import jax
import jax.numpy as jnp
from jax import lax
from jax.sharding import Mesh
from jax.sharding import PartitionSpec as P

AXES = ("x", "s", "p", "zh", "y", "c")
SIZES = (4, 4, 2, 2, 4, 2)


def split(value):
    high = lax.reduce_precision(value, 8, 7)
    return high.astype(jnp.bfloat16), (value - high).astype(jnp.bfloat16)


def contract(rows, weights):
    return lax.dot_general(
        rows, weights, (((1,), (1,)), ((), ())), preferred_element_type=jnp.float32
    )


def shift(value, axis, by):
    size = lax.axis_size(axis)
    return lax.ppermute(value, axis, [((i + by) % size, i) for i in range(size)])


def per_device(amplitudes, integrals):
    nx, ns, np_, nzh, ny, nc = SIZES
    rows, panels, _ = amplitudes.shape
    block, _, width = integrals.shape
    depth = panels * width
    x, p, c = (lax.axis_index(a) for a in ("x", "p", "c"))

    own = integrals.reshape(block, depth)
    pair = shift(own, "p", 1)
    pieces = {(0, 0): own, (1, 0): pair}
    for e, part in enumerate((own, pair)):
        for d in (1, nx - 1, 2):
            pieces[e, d] = shift(part, "x", d)
    swap = [(a * ny + b, b * nx + a) for a in range(nx) for b in range(ny)]
    moved = lax.ppermute(amplitudes, ("x", "y"), swap)
    moved, pieces[0, 0] = lax.optimization_barrier((moved, own))
    moved = moved.reshape(rows, panels, nzh, ny * nc, width).transpose(2, 3, 0, 1, 4)
    unit = rows * panels
    moved = moved.reshape(nzh, 1, ny * nc, unit, width)
    moved = jnp.broadcast_to(moved, (nzh, ns) + moved.shape[2:])
    moved = moved.reshape(nzh * ns * ny * nc, unit, width)
    held = lax.all_to_all(moved, ("zh", "s", "y", "c"), 0, 0, tiled=True)
    weights = None
    for (e, d), piece in pieces.items():
        place = np_ * ((x + d) & (nx - 1)) + (p ^ e)
        high, low = split(piece)
        piece = jnp.concatenate([high, low, high], axis=1)[None]
        if weights is None:
            weights = jnp.broadcast_to(piece, (nx * np_,) + piece.shape[1:])
        else:
            weights = lax.dynamic_update_slice_in_dim(weights, piece, place, 0)
    weights = weights.reshape(nx * np_ * block, 3 * depth)

    held = held.reshape(nzh, 2, 2, 2, 2, nc * unit, width)
    held = held.transpose(2, 4, 1, 3, 0, 5, 6).reshape(2, ny * nzh * nzh * nc * unit, width)
    group = nzh * nc * rows
    halves = []
    for index in (1 - c, c):
        half = lax.dynamic_index_in_dim(held, index, 0, keepdims=False)
        high, low = split(half.reshape(ny * nzh * group, depth))
        halves.append(jnp.concatenate([high, high, low], axis=1))

    away = contract(halves[0], weights)
    other = shift(away, "c", 1)
    home = lax.optimization_barrier(contract(halves[1], weights))
    home = home + other
    home = home.reshape(ny, nzh * group, home.shape[1])
    home = lax.all_to_all(home, "y", 0, 0, tiled=True)
    home = (home[0] + home[1]) + (home[2] + home[3])
    home = home.reshape(nzh, group, nx * np_, block).transpose(0, 2, 1, 3)
    home = home.reshape(nzh * nx * np_, group, block)
    out = lax.all_to_all(home, ("zh", "x", "p"), 0, 0, tiled=True)
    out = out.reshape(nzh, ny, np_, nzh, nc * rows, block)
    out = (out[0] + out[1]).transpose(1, 2, 0, 3, 4)
    return out.reshape(np_ * nzh * ny * nc * rows, block)


def solution(mesh):
    fine = Mesh(mesh.devices.reshape(SIZES), AXES)
    in_specs = (P(AXES, None, None), P(AXES[:3], None, AXES[3:]))
    out_specs = P(AXES[3:], AXES[:3])
    return jax.shard_map(
        per_device, mesh=fine, in_specs=in_specs, out_specs=out_specs, check_vma=False
    )
```

time: 192 us -> 160 us (0.83)
  the two profiles are of different devices: /device:TPU:32 before, /device:TPU:33 now
where the time goes in v3:
time: 160 us; the launch traced here: 159 us
  blocking collectives  63 us (39%)
  starting transfers between devices  46.5 us (29%)
  waiting for transfers between devices  23.4 us (15%)
  matrix products  11.1 us (7%)
  other arithmetic  7.7 us (5%)
  local copies, waits for them, and re-layouts  6.88 us (4%)
    all_to_all x1, blocking collectives, per_device(): out = lax.all_to_all(home, ('zh', 'x', 'p'), 0, 0, tiled=True)  40.1 us
    ppermute x8, starting transfers between devices, shift(): lax.ppermute(value, axis, [((i + by) % size, i) for i in range(size)])  26.7 us
    all_to_all x1, blocking collectives, per_device(): home = lax.all_to_all(home, 'y', 0, 0, tiled=True)  22.9 us
    ppermute x8, waiting for transfers between devices, shift(): lax.ppermute(value, axis, [((i + by) % size, i) for i in range(size)])  19.9 us
    all_to_all x1, starting transfers between devices, per_device(): held = lax.all_to_all(moved, ('zh', 's', 'y', 'c'), 0, 0, tiled=True)  18.2 us
    dot_general x2, matrix products, contract(): lax.dot_general(rows, weights, (((1,), (1,)), ((), ())), preferred_elemen...  11.1 us
    dynamic_update_slice x7, other arithmetic, per_device(): weights = lax.dynamic_update_slice_in_dim(weights, piece, place, 0)  6.64 us
    all_to_all x1, waiting for transfers between devices, per_device(): held = lax.all_to_all(moved, ('zh', 's', 'y', 'c'), 0, 0, tiled=True)  3.49 us
  transfers between devices with their start and end apart: 10, of which 3 were waited for; matrix products, arithmetic and copies ran while one was open for 11% of the time, Pallas kernels for 0%

profile of v3, /device:TPU:33, one launch (start us, length us, event | category | flops | bytes accessed | tf_op | source)
XLA Modules:
  0.0 158.9 jit_solution(1599144766721556804)
XLA Ops:
  0.0 1.6 collective-permute-start
  1.6 1.1 copy.15
  2.7 1.9 %collective-permute-start.1 = (f32[256,512]{1,0:T(8,128)S(1)}, f32[256,512]{1,0:T(8,128)S(1)}, u32[]{:S(2)}, u32[]{:S(2)}) collective-permute-start(f32[256,512]{1,0:T(8,128)S(1)} %bitcast.59), channel_id=1, source_target_pairs={{16,0},{0,16},{17,1},{1,17},{18,2},{2,18},{19,3},{3,19},{20,4},{4,... | collective-permute-start | bytes 1572872 | tf_op jit(solution)/shard_map/ppermute | solution.py:24
  4.6 7.4 %collective-permute-start.2 = (f32[256,512]{1,0:T(8,128)S(1)}, f32[256,512]{1,0:T(8,128)S(1)}, u32[]{:S(2)}, u32[]{:S(2)}) collective-permute-start(f32[256,512]{1,0:T(8,128)S(1)} %bitcast.60), channel_id=1, source_target_pairs={{128,0},{256,128},{384,256},{0,384},{129,1},{257,129},{385,257},{1... | collective-permute-start | bytes 1572872 | tf_op jit(solution)/shard_map/ppermute | solution.py:24
  12.0 1.9 %collective-permute-start.3 = (f32[256,512]{1,0:T(8,128)S(1)}, f32[256,512]{1,0:T(8,128)S(1)}, u32[]{:S(2)}, u32[]{:S(2)}) collective-permute-start(f32[256,512]{1,0:T(8,128)S(1)} %bitcast.61), channel_id=1, source_target_pairs={{384,0},{0,128},{128,256},{256,384},{385,1},{1,129},{129,257},{257... | collective-permute-start | bytes 1572872 | tf_op jit(solution)/shard_map/ppermute | solution.py:24
  13.9 3.8 %collective-permute-start.4 = (f32[256,512]{1,0:T(8,128)S(1)}, f32[256,512]{1,0:T(8,128)S(1)}, u32[]{:S(2)}, u32[]{:S(2)}) collective-permute-start(f32[256,512]{1,0:T(8,128)S(1)} %bitcast.62), channel_id=1, source_target_pairs={{256,0},{384,128},{0,256},{128,384},{257,1},{385,129},{1,257},{129... | collective-permute-start | bytes 1572872 | tf_op jit(solution)/shard_map/ppermute | solution.py:24
  17.8 0.0 collective-permute-done
  17.8 0.1 reshape.53
  17.9 0.1 copy.7
  18.0 1.0 broadcast_in_dim.35
  18.9 18.2 %all-to-all-start = ((f32[64,24,128]{2,1,0:T(8,128)}), f32[64,24,128]{2,1,0:T(8,128)S(1)}, u32[]{:S(2)}, u32[]{:S(2)}) async-start(f32[64,24,128]{2,1,0:T(8,128)} %bitcast.2), calls=%async_computation | async-start | bytes 1572864 | tf_op jit(solution)/shard_map/all_to_all | solution.py:48
  37.2 0.1 fusion.19
  37.2 0.1 pad_maximum_fusion
  37.3 0.0 collective-permute-done.1
  37.3 0.1 fusion.20
  37.4 3.2 %broadcast_in_dim.36 = bf16[8,256,1536]{2,1,0:T(8,128)(2,1)} broadcast(bf16[256,1536]{1,0:T(8,128)(2,1)S(1)} %pad_maximum_fusion), dimensions={1,2} | broadcast | bytes 7077888 | tf_op jit(solution)/shard_map/broadcast_in_dim | solution.py:55
  40.6 0.9 fusion
  41.5 0.0 collective-permute-done.2
  41.5 0.1 fusion.21
  41.6 0.9 fusion.1
  42.6 4.2 %collective-permute-start.5 = (f32[256,512]{1,0:T(8,128)S(1)}, f32[256,512]{1,0:T(8,128)S(1)}, u32[]{:S(2)}, u32[]{:S(2)}) collective-permute-start(f32[256,512]{1,0:T(8,128)S(1)} %collective-permute-done.1), channel_id=1, source_target_pairs={{128,0},{256,128},{384,256},{0,384},{129,1},{257,129},{385,257},{1... | collective-permute-start | bytes 1572872 | tf_op jit(solution)/shard_map/ppermute | solution.py:24
  46.8 0.0 collective-permute-done.3
  46.8 0.1 fusion.22
  46.9 1.0 fusion.2
  47.8 1.9 %collective-permute-start.6 = (f32[256,512]{1,0:T(8,128)S(1)}, f32[256,512]{1,0:T(8,128)S(1)}, u32[]{:S(2)}, u32[]{:S(2)}) collective-permute-start(f32[256,512]{1,0:T(8,128)S(1)} %collective-permute-done.1), channel_id=1, source_target_pairs={{384,0},{0,128},{128,256},{256,384},{385,1},{1,129},{129,257},{257... | collective-permute-start | bytes 1572872 | tf_op jit(solution)/shard_map/ppermute | solution.py:24
  49.8 0.0 collective-permute-done.4
  49.8 0.1 fusion.23
  49.8 0.9 fusion.3
  50.8 3.3 %collective-permute-start.7 = (f32[256,512]{1,0:T(8,128)S(1)}, f32[256,512]{1,0:T(8,128)S(1)}, u32[]{:S(2)}, u32[]{:S(2)}) collective-permute-start(f32[256,512]{1,0:T(8,128)S(1)} %collective-permute-done.1), channel_id=1, source_target_pairs={{256,0},{384,128},{0,256},{128,384},{257,1},{385,129},{1,257},{129... | collective-permute-start | bytes 1572872 | tf_op jit(solution)/shard_map/ppermute | solution.py:24
  54.1 4.1 %collective-permute-done.5 = f32[256,512]{1,0:T(8,128)S(1)} collective-permute-done((f32[256,512]{1,0:T(8,128)S(1)}, f32[256,512]{1,0:T(8,128)S(1)}, u32[]{:S(2)}, u32[]{:S(2)}) %collective-permute-start.5) | collective-permute-done | bytes 524320 | tf_op jit(solution)/shard_map/ppermute | solution.py:24
  58.2 0.1 fusion.24
  58.2 0.9 fusion.4
  59.2 15.7 %collective-permute-done.6 = f32[256,512]{1,0:T(8,128)S(1)} collective-permute-done((f32[256,512]{1,0:T(8,128)S(1)}, f32[256,512]{1,0:T(8,128)S(1)}, u32[]{:S(2)}, u32[]{:S(2)}) %collective-permute-start.6) | collective-permute-done | bytes 524320 | tf_op jit(solution)/shard_map/ppermute | solution.py:24
  74.9 0.1 fusion.25
  75.0 1.0 fusion.5
  75.9 0.0 collective-permute-done.7
  76.0 0.1 fusion.26
  76.0 0.9 fusion.6
  77.0 3.5 %all-to-all-done = f32[64,24,128]{2,1,0:T(8,128)S(1)} async-done(((f32[64,24,128]{2,1,0:T(8,128)}), f32[64,24,128]{2,1,0:T(8,128)S(1)}, u32[]{:S(2)}, u32[]{:S(2)}) %all-to-all-start) | async-done | bytes 786464 | tf_op jit(solution)/shard_map/all_to_all | solution.py:48
  80.5 0.1 copy.8
  80.6 0.1 constant_dynamic-slice_fusion
  80.6 0.1 reshape.59
  80.8 6.1 %fusion.13 = f32[192,2048]{1,0:T(8,128)} fusion(bf16[2048,1536]{1,0:T(8,128)(2,1)} %bitcast.13, bf16[192,512]{1,0:T(8,128)(2,1)S(1)} %get-tuple-element.28, bf16[192,512]{1,0:T(8,128)(2,1)S(1)} %get-tuple-element.27), kind=kOutput, calls=%fused_computation.37 | convolution fusion | flops 1209729024 | bytes 8257536 | tf_op jit(solution)/shard_map/dot_general | solution.py:17
  86.9 2.3 %collective-permute-start.8 = (f32[192,2048]{1,0:T(8,128)}, f32[192,2048]{1,0:T(8,128)S(1)}, u32[]{:S(2)}, u32[]{:S(2)}) collective-permute-start(f32[192,2048]{1,0:T(8,128)} %fusion.13), channel_id=1, source_target_pairs={{1,0},{0,1},{3,2},{2,3},{5,4},{4,5},{7,6},{6,7},{9,8},{8,9},{11,10... | collective-permute-start | bytes 4718600 | tf_op jit(solution)/shard_map/ppermute | solution.py:24
  89.2 0.1 reshape.57
  89.3 5.0 %fusion.7 = f32[192,2048]{1,0:T(8,128)S(1)} fusion(bf16[2048,1536]{1,0:T(8,128)(2,1)} %bitcast.13, bf16[192,512]{1,0:T(8,128)(2,1)S(1)} %get-tuple-element.30, bf16[192,512]{1,0:T(8,128)(2,1)S(1)} %get-tuple-element.29), kind=kOutput, calls=%fused_computation.31 | convolution fusion | flops 1209729024 | bytes 8257536 | tf_op jit(solution)/shard_map/dot_general | solution.py:17
  94.3 0.0 collective-permute-done.8
  94.3 0.2 add.107
  94.5 22.9 %all_to_all.15 = f32[4,48,2048]{2,1,0:T(8,128)S(1)} all-to-all(f32[4,48,2048]{2,1,0:T(8,128)S(1)} %bitcast.56), channel_id=1, replica_groups=mesh['x'=4,'s'=4,'p'=2,'zh'=2,'y'=4,'c'=2] {'y'}, dimensions={0} | all-to-all | bytes 3145728 | tf_op jit(solution)/shard_map/all_to_all | solution.py:74
  117.4 0.1 fusion.29
  117.5 0.1 copy.13
  117.6 0.1 copy.9
  117.8 40.1 %all_to_all.16 = f32[16,24,256]{2,1,0:T(8,128)S(1)} all-to-all(f32[16,24,256]{2,1,0:T(8,128)S(1)} %bitcast.65), channel_id=1, replica_groups=mesh['x'=4,'s'=4,'p'=2,'zh'=2,'y'=4,'c'=2] {'zh','x','p'}, dimensions={0} | all-to-all | bytes 786432 | tf_op jit(solution)/shard_map/all_to_all | solution.py:78
  157.9 0.1 copy.10
  158.0 0.1 add.113
  158.1 0.1 copy.11
  158.2 0.7 reshape.62
  (4 shorter events, 0.1 us)
Async XLA Ops:
  0.0 17.8 %collective-permute-start = (f32[6,4,2048]{2,1,0:T(4,128)}, f32[6,4,2048]{2,1,0:T(4,128)S(1)}, u32[]{:S(2)}, u32[]{:S(2)}) collective-permute-start(f32[6,4,2048]{2,1,0:T(4,128)} %param.2), channel_id=1, source_target_pairs={{0,0},{2,128},{4,256},{6,384},{128,2},{130,130},{132,258},{134,386... | collective-permute-start | bytes 589832 | tf_op jit(solution)/shard_map/ppermute | solution.py:41
  2.7 34.7 %collective-permute-start.1 = (f32[256,512]{1,0:T(8,128)S(1)}, f32[256,512]{1,0:T(8,128)S(1)}, u32[]{:S(2)}, u32[]{:S(2)}) collective-permute-start(f32[256,512]{1,0:T(8,128)S(1)} %bitcast.59), channel_id=1, source_target_pairs={{16,0},{0,16},{17,1},{1,17},{18,2},{2,18},{19,3},{3,19},{20,4},{4,... | collective-permute-start | bytes 1572872 | tf_op jit(solution)/shard_map/ppermute | solution.py:24
  4.6 37.0 %collective-permute-start.2 = (f32[256,512]{1,0:T(8,128)S(1)}, f32[256,512]{1,0:T(8,128)S(1)}, u32[]{:S(2)}, u32[]{:S(2)}) collective-permute-start(f32[256,512]{1,0:T(8,128)S(1)} %bitcast.60), channel_id=1, source_target_pairs={{128,0},{256,128},{384,256},{0,384},{129,1},{257,129},{385,257},{1... | collective-permute-start | bytes 1572872 | tf_op jit(solution)/shard_map/ppermute | solution.py:24
  12.0 34.8 %collective-permute-start.3 = (f32[256,512]{1,0:T(8,128)S(1)}, f32[256,512]{1,0:T(8,128)S(1)}, u32[]{:S(2)}, u32[]{:S(2)}) collective-permute-start(f32[256,512]{1,0:T(8,128)S(1)} %bitcast.61), channel_id=1, source_target_pairs={{384,0},{0,128},{128,256},{256,384},{385,1},{1,129},{129,257},{257... | collective-permute-start | bytes 1572872 | tf_op jit(solution)/shard_map/ppermute | solution.py:24
  13.9 35.9 %collective-permute-start.4 = (f32[256,512]{1,0:T(8,128)S(1)}, f32[256,512]{1,0:T(8,128)S(1)}, u32[]{:S(2)}, u32[]{:S(2)}) collective-permute-start(f32[256,512]{1,0:T(8,128)S(1)} %bitcast.62), channel_id=1, source_target_pairs={{256,0},{384,128},{0,256},{128,384},{257,1},{385,129},{1,257},{129... | collective-permute-start | bytes 1572872 | tf_op jit(solution)/shard_map/ppermute | solution.py:24
  18.9 61.5 %all-to-all-start = ((f32[64,24,128]{2,1,0:T(8,128)}), f32[64,24,128]{2,1,0:T(8,128)S(1)}, u32[]{:S(2)}, u32[]{:S(2)}) async-start(f32[64,24,128]{2,1,0:T(8,128)} %bitcast.2), calls=%async_computation | async-start | bytes 1572864 | tf_op jit(solution)/shard_map/all_to_all | solution.py:48
  42.6 15.6 %collective-permute-start.5 = (f32[256,512]{1,0:T(8,128)S(1)}, f32[256,512]{1,0:T(8,128)S(1)}, u32[]{:S(2)}, u32[]{:S(2)}) collective-permute-start(f32[256,512]{1,0:T(8,128)S(1)} %collective-permute-done.1), channel_id=1, source_target_pairs={{128,0},{256,128},{384,256},{0,384},{129,1},{257,129},{385,257},{1... | collective-permute-start | bytes 1572872 | tf_op jit(solution)/shard_map/ppermute | solution.py:24
  47.8 27.1 %collective-permute-start.6 = (f32[256,512]{1,0:T(8,128)S(1)}, f32[256,512]{1,0:T(8,128)S(1)}, u32[]{:S(2)}, u32[]{:S(2)}) collective-permute-start(f32[256,512]{1,0:T(8,128)S(1)} %collective-permute-done.1), channel_id=1, source_target_pairs={{384,0},{0,128},{128,256},{256,384},{385,1},{1,129},{129,257},{257... | collective-permute-start | bytes 1572872 | tf_op jit(solution)/shard_map/ppermute | solution.py:24
  50.8 25.2 %collective-permute-start.7 = (f32[256,512]{1,0:T(8,128)S(1)}, f32[256,512]{1,0:T(8,128)S(1)}, u32[]{:S(2)}, u32[]{:S(2)}) collective-permute-start(f32[256,512]{1,0:T(8,128)S(1)} %collective-permute-done.1), channel_id=1, source_target_pairs={{256,0},{384,128},{0,256},{128,384},{257,1},{385,129},{1,257},{129... | collective-permute-start | bytes 1572872 | tf_op jit(solution)/shard_map/ppermute | solution.py:24
  86.9 7.4 %collective-permute-start.8 = (f32[192,2048]{1,0:T(8,128)}, f32[192,2048]{1,0:T(8,128)S(1)}, u32[]{:S(2)}, u32[]{:S(2)}) collective-permute-start(f32[192,2048]{1,0:T(8,128)} %fusion.13), channel_id=1, source_target_pairs={{1,0},{0,1},{3,2},{2,3},{5,4},{4,5},{7,6},{6,7},{9,8},{8,9},{11,10... | collective-permute-start | bytes 4718600 | tf_op jit(solution)/shard_map/ppermute | solution.py:24

commit v4 on v3

--- a/solution.py
+++ b/solution.py
@@ -40,12 +40,12 @@
     swap = [(a * ny + b, b * nx + a) for a in range(nx) for b in range(ny)]
     moved = lax.ppermute(amplitudes, ("x", "y"), swap)
     moved, pieces[0, 0] = lax.optimization_barrier((moved, own))
-    moved = moved.reshape(rows, panels, nzh, ny * nc, width).transpose(2, 3, 0, 1, 4)
+    moved = moved.reshape(rows, panels, nzh, ny * nc, width).transpose(3, 2, 0, 1, 4)
     unit = rows * panels
-    moved = moved.reshape(nzh, 1, ny * nc, unit, width)
-    moved = jnp.broadcast_to(moved, (nzh, ns) + moved.shape[2:])
-    moved = moved.reshape(nzh * ns * ny * nc, unit, width)
-    held = lax.all_to_all(moved, ("zh", "s", "y", "c"), 0, 0, tiled=True)
+    moved = moved.reshape(ny * nc, 1, nzh, unit, width)
+    moved = jnp.broadcast_to(moved, (ny * nc, ns, nzh, unit, width))
+    moved = moved.reshape(ny * nc * ns * nzh, unit, width)
+    held = lax.all_to_all(moved, ("y", "c", "s", "zh"), 0, 0, tiled=True)
     weights = None
     for (e, d), piece in pieces.items():
         place = np_ * ((x + d) & (nx - 1)) + (p ^ e)
@@ -57,8 +57,9 @@
             weights = lax.dynamic_update_slice_in_dim(weights, piece, place, 0)
     weights = weights.reshape(nx * np_ * block, 3 * depth)
 
-    held = held.reshape(nzh, 2, 2, 2, 2, nc * unit, width)
-    held = held.transpose(2, 4, 1, 3, 0, 5, 6).reshape(2, ny * nzh * nzh * nc * unit, width)
+    held = held.reshape(2, 2, nc, 2, 2, nzh, unit, width)
+    held = held.transpose(4, 1, 3, 0, 5, 2, 6, 7)
+    held = held.reshape(2, ny * nzh * nzh * nc * unit, width)
     group = nzh * nc * rows
     halves = []
     for index in (1 - c, c):
@@ -73,11 +74,11 @@
     home = home.reshape(ny, nzh * group, home.shape[1])
     home = lax.all_to_all(home, "y", 0, 0, tiled=True)
     home = (home[0] + home[1]) + (home[2] + home[3])
-    home = home.reshape(nzh, group, nx * np_, block).transpose(0, 2, 1, 3)
-    home = home.reshape(nzh * nx * np_, group, block)
-    out = lax.all_to_all(home, ("zh", "x", "p"), 0, 0, tiled=True)
-    out = out.reshape(nzh, ny, np_, nzh, nc * rows, block)
-    out = (out[0] + out[1]).transpose(1, 2, 0, 3, 4)
+    home = home.reshape(nzh, group, nx * np_, block).transpose(2, 0, 1, 3)
+    home = home.reshape(nx * np_ * nzh, group, block)
+    out = lax.all_to_all(home, ("x", "p", "zh"), 0, 0, tiled=True)
+    out = out.reshape(ny, np_, nzh, nzh, nc * rows, block)
+    out = (out[:, :, 0] + out[:, :, 1]).transpose(1, 2, 0, 3, 4)
     return out.reshape(np_ * nzh * ny * nc * rows, block)
 
 

time: 160 us -> 160 us (level)
  the two profiles are of different devices: /device:TPU:33 before, /device:TPU:32 now
where the time goes in v4:
time: 160 us; the launch traced here: 159 us
  blocking collectives  65.1 us (41%)
  starting transfers between devices  46.5 us (29%)
  waiting for transfers between devices  21.3 us (13%)
  matrix products  11.1 us (7%)
  other arithmetic  7.88 us (5%)
  local copies, waits for them, and re-layouts  7.18 us (4%)
    all_to_all x1, blocking collectives, per_device(): out = lax.all_to_all(home, ('x', 'p', 'zh'), 0, 0, tiled=True)  40.2 us
    ppermute x8, starting transfers between devices, shift(): lax.ppermute(value, axis, [((i + by) % size, i) for i in range(size)])  28.1 us
    all_to_all x1, blocking collectives, per_device(): home = lax.all_to_all(home, 'y', 0, 0, tiled=True)  24.9 us
    ppermute x8, waiting for transfers between devices, shift(): lax.ppermute(value, axis, [((i + by) % size, i) for i in range(size)])  20.4 us
    all_to_all x1, starting transfers between devices, per_device(): held = lax.all_to_all(moved, ('y', 'c', 's', 'zh'), 0, 0, tiled=True)  16.8 us
    dot_general x2, matrix products, contract(): lax.dot_general(rows, weights, (((1,), (1,)), ((), ())), preferred_elemen...  11.1 us
    dynamic_update_slice x7, other arithmetic, per_device(): weights = lax.dynamic_update_slice_in_dim(weights, piece, place, 0)  6.64 us
  transfers between devices with their start and end apart: 10, of which 3 were waited for; matrix products, arithmetic and copies ran while one was open for 11% of the time, Pallas kernels for 0%

profile of v4, /device:TPU:32, one launch (start us, length us, event | category | flops | bytes accessed | tf_op | source)
XLA Modules:
  0.0 159.4 jit_solution(11063255979233780513)
XLA Ops:
  0.0 1.6 collective-permute-start
  1.6 1.1 copy.17
  2.7 7.4 %collective-permute-start.1 = (f32[256,512]{1,0:T(8,128)S(1)}, f32[256,512]{1,0:T(8,128)S(1)}, u32[]{:S(2)}, u32[]{:S(2)}) collective-permute-start(f32[256,512]{1,0:T(8,128)S(1)} %bitcast.63), channel_id=1, source_target_pairs={{16,0},{0,16},{17,1},{1,17},{18,2},{2,18},{19,3},{3,19},{20,4},{4,... | collective-permute-start | bytes 1572872 | tf_op jit(solution)/shard_map/ppermute | solution.py:24
  10.0 2.6 %collective-permute-start.2 = (f32[256,512]{1,0:T(8,128)S(1)}, f32[256,512]{1,0:T(8,128)S(1)}, u32[]{:S(2)}, u32[]{:S(2)}) collective-permute-start(f32[256,512]{1,0:T(8,128)S(1)} %bitcast.64), channel_id=1, source_target_pairs={{128,0},{256,128},{384,256},{0,384},{129,1},{257,129},{385,257},{1... | collective-permute-start | bytes 1572872 | tf_op jit(solution)/shard_map/ppermute | solution.py:24
  12.6 3.3 %collective-permute-start.3 = (f32[256,512]{1,0:T(8,128)S(1)}, f32[256,512]{1,0:T(8,128)S(1)}, u32[]{:S(2)}, u32[]{:S(2)}) collective-permute-start(f32[256,512]{1,0:T(8,128)S(1)} %bitcast.65), channel_id=1, source_target_pairs={{384,0},{0,128},{128,256},{256,384},{385,1},{1,129},{129,257},{257... | collective-permute-start | bytes 1572872 | tf_op jit(solution)/shard_map/ppermute | solution.py:24
  15.9 3.1 %collective-permute-start.4 = (f32[256,512]{1,0:T(8,128)S(1)}, f32[256,512]{1,0:T(8,128)S(1)}, u32[]{:S(2)}, u32[]{:S(2)}) collective-permute-start(f32[256,512]{1,0:T(8,128)S(1)} %bitcast.66), channel_id=1, source_target_pairs={{256,0},{384,128},{0,256},{128,384},{257,1},{385,129},{1,257},{129... | collective-permute-start | bytes 1572872 | tf_op jit(solution)/shard_map/ppermute | solution.py:24
  19.0 0.0 collective-permute-done
  19.0 0.1 reshape.51
  19.1 0.1 copy.7
  19.2 1.0 broadcast_in_dim.35
  20.1 16.8 %all-to-all-start = ((f32[64,24,128]{2,1,0:T(8,128)}), f32[64,24,128]{2,1,0:T(8,128)S(1)}, u32[]{:S(2)}, u32[]{:S(2)}) async-start(f32[64,24,128]{2,1,0:T(8,128)} %bitcast.2), calls=%async_computation | async-start | bytes 1572864 | tf_op jit(solution)/shard_map/all_to_all | solution.py:48
  36.9 0.1 fusion.19
  37.0 0.1 pad_maximum_fusion
  37.1 0.0 collective-permute-done.1
  37.1 0.1 fusion.20
  37.2 3.2 %broadcast_in_dim.36 = bf16[8,256,1536]{2,1,0:T(8,128)(2,1)} broadcast(bf16[256,1536]{1,0:T(8,128)(2,1)S(1)} %pad_maximum_fusion), dimensions={1,2} | broadcast | bytes 7077888 | tf_op jit(solution)/shard_map/broadcast_in_dim | solution.py:55
  40.4 0.9 fusion
  41.3 0.0 collective-permute-done.2
  41.3 0.1 fusion.21
  41.4 0.9 fusion.1
  42.3 4.5 %collective-permute-start.5 = (f32[256,512]{1,0:T(8,128)S(1)}, f32[256,512]{1,0:T(8,128)S(1)}, u32[]{:S(2)}, u32[]{:S(2)}) collective-permute-start(f32[256,512]{1,0:T(8,128)S(1)} %collective-permute-done.1), channel_id=1, source_target_pairs={{128,0},{256,128},{384,256},{0,384},{129,1},{257,129},{385,257},{1... | collective-permute-start | bytes 1572872 | tf_op jit(solution)/shard_map/ppermute | solution.py:24
  46.9 0.0 collective-permute-done.3
  46.9 0.1 fusion.22
  46.9 1.0 fusion.2
  47.9 1.9 %collective-permute-start.6 = (f32[256,512]{1,0:T(8,128)S(1)}, f32[256,512]{1,0:T(8,128)S(1)}, u32[]{:S(2)}, u32[]{:S(2)}) collective-permute-start(f32[256,512]{1,0:T(8,128)S(1)} %collective-permute-done.1), channel_id=1, source_target_pairs={{384,0},{0,128},{128,256},{256,384},{385,1},{1,129},{129,257},{257... | collective-permute-start | bytes 1572872 | tf_op jit(solution)/shard_map/ppermute | solution.py:24
  49.8 0.0 collective-permute-done.4
  49.8 0.1 fusion.23
  49.9 0.9 fusion.3
  50.9 3.5 %collective-permute-start.7 = (f32[256,512]{1,0:T(8,128)S(1)}, f32[256,512]{1,0:T(8,128)S(1)}, u32[]{:S(2)}, u32[]{:S(2)}) collective-permute-start(f32[256,512]{1,0:T(8,128)S(1)} %collective-permute-done.1), channel_id=1, source_target_pairs={{256,0},{384,128},{0,256},{128,384},{257,1},{385,129},{1,257},{129... | collective-permute-start | bytes 1572872 | tf_op jit(solution)/shard_map/ppermute | solution.py:24
  54.4 15.1 %collective-permute-done.5 = f32[256,512]{1,0:T(8,128)S(1)} collective-permute-done((f32[256,512]{1,0:T(8,128)S(1)}, f32[256,512]{1,0:T(8,128)S(1)}, u32[]{:S(2)}, u32[]{:S(2)}) %collective-permute-start.5) | collective-permute-done | bytes 524320 | tf_op jit(solution)/shard_map/ppermute | solution.py:24
  69.5 0.1 fusion.24
  69.6 0.9 fusion.4
  70.5 5.3 %collective-permute-done.6 = f32[256,512]{1,0:T(8,128)S(1)} collective-permute-done((f32[256,512]{1,0:T(8,128)S(1)}, f32[256,512]{1,0:T(8,128)S(1)}, u32[]{:S(2)}, u32[]{:S(2)}) %collective-permute-start.6) | collective-permute-done | bytes 524320 | tf_op jit(solution)/shard_map/ppermute | solution.py:24
  75.8 0.1 fusion.25
  75.9 1.0 fusion.5
  76.9 0.0 collective-permute-done.7
  76.9 0.1 fusion.26
  77.0 0.9 fusion.6
  77.9 0.8 all-to-all-done
  78.7 0.1 copy.8
  78.8 0.1 constant_dynamic-slice_fusion
  78.9 0.1 reshape.57
  79.0 6.1 %fusion.13 = f32[192,2048]{1,0:T(8,128)} fusion(bf16[2048,1536]{1,0:T(8,128)(2,1)} %bitcast.13, bf16[192,512]{1,0:T(8,128)(2,1)S(1)} %get-tuple-element.28, bf16[192,512]{1,0:T(8,128)(2,1)S(1)} %get-tuple-element.27), kind=kOutput, calls=%fused_computation.37 | convolution fusion | flops 1209729024 | bytes 8257536 | tf_op jit(solution)/shard_map/dot_general | solution.py:17
  85.1 1.9 %collective-permute-start.8 = (f32[192,2048]{1,0:T(8,128)}, f32[192,2048]{1,0:T(8,128)S(1)}, u32[]{:S(2)}, u32[]{:S(2)}) collective-permute-start(f32[192,2048]{1,0:T(8,128)} %fusion.13), channel_id=1, source_target_pairs={{1,0},{0,1},{3,2},{2,3},{5,4},{4,5},{7,6},{6,7},{9,8},{8,9},{11,10... | collective-permute-start | bytes 4718600 | tf_op jit(solution)/shard_map/ppermute | solution.py:24
  87.0 0.1 reshape.55
  87.2 5.0 %fusion.7 = f32[192,2048]{1,0:T(8,128)S(1)} fusion(bf16[2048,1536]{1,0:T(8,128)(2,1)} %bitcast.13, bf16[192,512]{1,0:T(8,128)(2,1)S(1)} %get-tuple-element.30, bf16[192,512]{1,0:T(8,128)(2,1)S(1)} %get-tuple-element.29), kind=kOutput, calls=%fused_computation.31 | convolution fusion | flops 1209729024 | bytes 8257536 | tf_op jit(solution)/shard_map/dot_general | solution.py:17
  92.1 0.0 collective-permute-done.8
  92.1 0.2 add.107
  92.4 24.9 %all_to_all.15 = f32[4,48,2048]{2,1,0:T(8,128)S(1)} all-to-all(f32[4,48,2048]{2,1,0:T(8,128)S(1)} %bitcast.60), channel_id=1, replica_groups=mesh['x'=4,'s'=4,'p'=2,'zh'=2,'y'=4,'c'=2] {'y'}, dimensions={0} | all-to-all | bytes 3145728 | tf_op jit(solution)/shard_map/all_to_all | solution.py:75
  117.3 0.1 fusion.29
  117.4 0.1 copy.14
  117.5 0.1 copy.9
  117.7 40.2 %all_to_all.16 = f32[16,24,256]{2,1,0:T(8,128)S(1)} all-to-all(f32[16,24,256]{2,1,0:T(8,128)S(1)} %bitcast.69), channel_id=1, replica_groups=mesh['x'=4,'s'=4,'p'=2,'zh'=2,'y'=4,'c'=2] {'x','p','zh'}, dimensions={0} | all-to-all | bytes 786432 | tf_op jit(solution)/shard_map/all_to_all | solution.py:79
  157.9 0.1 copy.10
  158.0 0.2 reshape.60
  158.3 0.2 slice_add_fusion.2
  158.5 0.1 copy.18
  158.6 0.1 copy.11
  158.7 0.7 reshape.61
  (3 shorter events, 0.1 us)
Async XLA Ops:
  0.0 19.0 %collective-permute-start = (f32[6,4,2048]{2,1,0:T(4,128)}, f32[6,4,2048]{2,1,0:T(4,128)S(1)}, u32[]{:S(2)}, u32[]{:S(2)}) collective-permute-start(f32[6,4,2048]{2,1,0:T(4,128)} %param.2), channel_id=1, source_target_pairs={{0,0},{2,128},{4,256},{6,384},{128,2},{130,130},{132,258},{134,386... | collective-permute-start | bytes 589832 | tf_op jit(solution)/shard_map/ppermute | solution.py:41
  2.7 34.4 %collective-permute-start.1 = (f32[256,512]{1,0:T(8,128)S(1)}, f32[256,512]{1,0:T(8,128)S(1)}, u32[]{:S(2)}, u32[]{:S(2)}) collective-permute-start(f32[256,512]{1,0:T(8,128)S(1)} %bitcast.63), channel_id=1, source_target_pairs={{16,0},{0,16},{17,1},{1,17},{18,2},{2,18},{19,3},{3,19},{20,4},{4,... | collective-permute-start | bytes 1572872 | tf_op jit(solution)/shard_map/ppermute | solution.py:24
  10.0 31.3 %collective-permute-start.2 = (f32[256,512]{1,0:T(8,128)S(1)}, f32[256,512]{1,0:T(8,128)S(1)}, u32[]{:S(2)}, u32[]{:S(2)}) collective-permute-start(f32[256,512]{1,0:T(8,128)S(1)} %bitcast.64), channel_id=1, source_target_pairs={{128,0},{256,128},{384,256},{0,384},{129,1},{257,129},{385,257},{1... | collective-permute-start | bytes 1572872 | tf_op jit(solution)/shard_map/ppermute | solution.py:24
  12.6 34.2 %collective-permute-start.3 = (f32[256,512]{1,0:T(8,128)S(1)}, f32[256,512]{1,0:T(8,128)S(1)}, u32[]{:S(2)}, u32[]{:S(2)}) collective-permute-start(f32[256,512]{1,0:T(8,128)S(1)} %bitcast.65), channel_id=1, source_target_pairs={{384,0},{0,128},{128,256},{256,384},{385,1},{1,129},{129,257},{257... | collective-permute-start | bytes 1572872 | tf_op jit(solution)/shard_map/ppermute | solution.py:24
  15.9 33.9 %collective-permute-start.4 = (f32[256,512]{1,0:T(8,128)S(1)}, f32[256,512]{1,0:T(8,128)S(1)}, u32[]{:S(2)}, u32[]{:S(2)}) collective-permute-start(f32[256,512]{1,0:T(8,128)S(1)} %bitcast.66), channel_id=1, source_target_pairs={{256,0},{384,128},{0,256},{128,384},{257,1},{385,129},{1,257},{129... | collective-permute-start | bytes 1572872 | tf_op jit(solution)/shard_map/ppermute | solution.py:24
  20.1 58.6 %all-to-all-start = ((f32[64,24,128]{2,1,0:T(8,128)}), f32[64,24,128]{2,1,0:T(8,128)S(1)}, u32[]{:S(2)}, u32[]{:S(2)}) async-start(f32[64,24,128]{2,1,0:T(8,128)} %bitcast.2), calls=%async_computation | async-start | bytes 1572864 | tf_op jit(solution)/shard_map/all_to_all | solution.py:48
  42.3 27.2 %collective-permute-start.5 = (f32[256,512]{1,0:T(8,128)S(1)}, f32[256,512]{1,0:T(8,128)S(1)}, u32[]{:S(2)}, u32[]{:S(2)}) collective-permute-start(f32[256,512]{1,0:T(8,128)S(1)} %collective-permute-done.1), channel_id=1, source_target_pairs={{128,0},{256,128},{384,256},{0,384},{129,1},{257,129},{385,257},{1... | collective-permute-start | bytes 1572872 | tf_op jit(solution)/shard_map/ppermute | solution.py:24
  47.9 27.9 %collective-permute-start.6 = (f32[256,512]{1,0:T(8,128)S(1)}, f32[256,512]{1,0:T(8,128)S(1)}, u32[]{:S(2)}, u32[]{:S(2)}) collective-permute-start(f32[256,512]{1,0:T(8,128)S(1)} %collective-permute-done.1), channel_id=1, source_target_pairs={{384,0},{0,128},{128,256},{256,384},{385,1},{1,129},{129,257},{257... | collective-permute-start | bytes 1572872 | tf_op jit(solution)/shard_map/ppermute | solution.py:24
  50.9 26.0 %collective-permute-start.7 = (f32[256,512]{1,0:T(8,128)S(1)}, f32[256,512]{1,0:T(8,128)S(1)}, u32[]{:S(2)}, u32[]{:S(2)}) collective-permute-start(f32[256,512]{1,0:T(8,128)S(1)} %collective-permute-done.1), channel_id=1, source_target_pairs={{256,0},{384,128},{0,256},{128,384},{257,1},{385,129},{1,257},{129... | collective-permute-start | bytes 1572872 | tf_op jit(solution)/shard_map/ppermute | solution.py:24
  85.1 7.0 %collective-permute-start.8 = (f32[192,2048]{1,0:T(8,128)}, f32[192,2048]{1,0:T(8,128)S(1)}, u32[]{:S(2)}, u32[]{:S(2)}) collective-permute-start(f32[192,2048]{1,0:T(8,128)} %fusion.13), channel_id=1, source_target_pairs={{1,0},{0,1},{3,2},{2,3},{5,4},{4,5},{7,6},{6,7},{9,8},{8,9},{11,10... | collective-permute-start | bytes 4718600 | tf_op jit(solution)/shard_map/ppermute | solution.py:24

commit v5 on v4

--- a/solution.py
+++ b/solution.py
@@ -35,8 +35,11 @@
     pair = shift(own, "p", 1)
     pieces = {(0, 0): own, (1, 0): pair}
     for e, part in enumerate((own, pair)):
-        for d in (1, nx - 1, 2):
+        for d in (1, nx - 1):
             pieces[e, d] = shift(part, "x", d)
+        low = shift(pieces[e, 1][: block // 2], "x", 1)
+        high = shift(pieces[e, nx - 1][block // 2 :], "x", nx - 1)
+        pieces[e, 2] = jnp.concatenate([low, high], axis=0)
     swap = [(a * ny + b, b * nx + a) for a in range(nx) for b in range(ny)]
     moved = lax.ppermute(amplitudes, ("x", "y"), swap)
     moved, pieces[0, 0] = lax.optimization_barrier((moved, own))

time: 160 us -> 160 us (level)
  waiting for transfers between devices: 21.3 us -> 12.9 us
  starting transfers between devices: 46.5 us -> 54.2 us
    ppermute x8 -> x10, waiting for transfers between devices: 20.4 us -> 12.9 us  [shift(): lax.ppermute(value, axis, [((i + by) % size, i) for i in range(size)])]
    ppermute x8 -> x10, starting transfers between devices: 28.1 us -> 34.1 us  [shift(): lax.ppermute(value, axis, [((i + by) % size, i) for i in range(size)])]
    all_to_all x1, starting transfers between devices: 16.8 us -> 18.6 us  [per_device(): held = lax.all_to_all(moved, ('y', 'c', 's', 'zh'), 0, 0, tiled=True)]
  transfers between devices with their start and end apart: 10 -> 12, of which waited for: 3 -> 3; matrix products, arithmetic and copies ran while one was open for 11% -> 11% of each run, Pallas kernels for 0% -> 0%
where the time goes in v5:
time: 160 us
  blocking collectives  66 us (41%)
  starting transfers between devices  54.2 us (34%)
  waiting for transfers between devices  12.9 us (8%)
  matrix products  11.1 us (7%)
  other arithmetic  7.92 us (5%)
  local copies, waits for them, and re-layouts  7.3 us (5%)
    all_to_all x1, blocking collectives, per_device(): out = lax.all_to_all(home, ('x', 'p', 'zh'), 0, 0, tiled=True)  40.2 us
    ppermute x10, starting transfers between devices, shift(): lax.ppermute(value, axis, [((i + by) % size, i) for i in range(size)])  34.1 us
    all_to_all x1, blocking collectives, per_device(): home = lax.all_to_all(home, 'y', 0, 0, tiled=True)  25.8 us
    all_to_all x1, starting transfers between devices, per_device(): held = lax.all_to_all(moved, ('y', 'c', 's', 'zh'), 0, 0, tiled=True)  18.6 us
    ppermute x10, waiting for transfers between devices, shift(): lax.ppermute(value, axis, [((i + by) % size, i) for i in range(size)])  12.9 us
    dot_general x2, matrix products, contract(): lax.dot_general(rows, weights, (((1,), (1,)), ((), ())), preferred_elemen...  11.1 us
    dynamic_update_slice x7, other arithmetic, per_device(): weights = lax.dynamic_update_slice_in_dim(weights, piece, place, 0)  6.67 us
  transfers between devices with their start and end apart: 12, of which 3 were waited for; matrix products, arithmetic and copies ran while one was open for 11% of the time, Pallas kernels for 0%

profile of v5, /device:TPU:32, one launch (start us, length us, event | category | flops | bytes accessed | tf_op | source)
XLA Modules:
  0.0 159.8 jit_solution(14631329378710536372)
XLA Ops:
  0.0 1.6 collective-permute-start
  1.6 1.1 copy.17
  2.7 7.9 %collective-permute-start.2 = (f32[256,512]{1,0:T(8,128)S(1)}, f32[256,512]{1,0:T(8,128)S(1)}, u32[]{:S(2)}, u32[]{:S(2)}) collective-permute-start(f32[256,512]{1,0:T(8,128)S(1)} %bitcast.63), channel_id=1, source_target_pairs={{128,0},{256,128},{384,256},{0,384},{129,1},{257,129},{385,257},{1... | collective-permute-start | bytes 1572872 | tf_op jit(solution)/shard_map/ppermute | solution.py:24
  10.6 1.9 %collective-permute-start.3 = (f32[256,512]{1,0:T(8,128)S(1)}, f32[256,512]{1,0:T(8,128)S(1)}, u32[]{:S(2)}, u32[]{:S(2)}) collective-permute-start(f32[256,512]{1,0:T(8,128)S(1)} %bitcast.64), channel_id=1, source_target_pairs={{384,0},{0,128},{128,256},{256,384},{385,1},{1,129},{129,257},{257... | collective-permute-start | bytes 1572872 | tf_op jit(solution)/shard_map/ppermute | solution.py:24
  12.5 3.4 %collective-permute-start.1 = (f32[256,512]{1,0:T(8,128)S(1)}, f32[256,512]{1,0:T(8,128)S(1)}, u32[]{:S(2)}, u32[]{:S(2)}) collective-permute-start(f32[256,512]{1,0:T(8,128)S(1)} %bitcast.65), channel_id=1, source_target_pairs={{16,0},{0,16},{17,1},{1,17},{18,2},{2,18},{19,3},{3,19},{20,4},{4,... | collective-permute-start | bytes 1572872 | tf_op jit(solution)/shard_map/ppermute | solution.py:24
  15.9 0.0 collective-permute-done
  15.9 0.1 reshape.51
  16.0 0.1 copy.7
  16.1 0.9 broadcast_in_dim.35
  17.1 18.6 %all-to-all-start = ((f32[64,24,128]{2,1,0:T(8,128)}), f32[64,24,128]{2,1,0:T(8,128)S(1)}, u32[]{:S(2)}, u32[]{:S(2)}) async-start(f32[64,24,128]{2,1,0:T(8,128)} %bitcast.2), calls=%async_computation | async-start | bytes 1572864 | tf_op jit(solution)/shard_map/all_to_all | solution.py:51
  35.6 0.1 fusion.19
  35.7 0.1 pad_maximum_fusion
  35.8 0.0 collective-permute-done.2
  35.8 2.8 %collective-permute-start.4 = (f32[128,512]{1,0:T(8,128)S(1)}, f32[128,512]{1,0:T(8,128)S(1)}, u32[]{:S(2)}, u32[]{:S(2)}) collective-permute-start(f32[128,512]{1,0:T(8,128)S(1)} %slice.40), channel_id=1, source_target_pairs={{128,0},{256,128},{384,256},{0,384},{129,1},{257,129},{385,257},{1... | collective-permute-start | bytes 786440 | tf_op jit(solution)/shard_map/ppermute | solution.py:24
  38.6 0.0 collective-permute-done.3
  38.6 3.1 %collective-permute-start.5 = (f32[128,512]{1,0:T(8,128)S(1)}, f32[128,512]{1,0:T(8,128)S(1)}, u32[]{:S(2)}, u32[]{:S(2)}) collective-permute-start(f32[128,512]{1,0:T(8,128)S(1)} %slice.41), channel_id=1, source_target_pairs={{384,0},{0,128},{128,256},{256,384},{385,1},{1,129},{129,257},{257... | collective-permute-start | bytes 786440 | tf_op jit(solution)/shard_map/ppermute | solution.py:24
  41.7 0.0 collective-permute-done.1
  41.7 0.1 fusion.20
  41.8 3.2 %broadcast_in_dim.36 = bf16[8,256,1536]{2,1,0:T(8,128)(2,1)} broadcast(bf16[256,1536]{1,0:T(8,128)(2,1)S(1)} %pad_maximum_fusion), dimensions={1,2} | broadcast | bytes 7077888 | tf_op jit(solution)/shard_map/broadcast_in_dim | solution.py:58
  45.0 0.9 fusion
  45.9 0.1 fusion.21
  46.0 1.0 fusion.1
  47.0 0.1 fusion.22
  47.0 4.0 %collective-permute-start.6 = (f32[256,512]{1,0:T(8,128)S(1)}, f32[256,512]{1,0:T(8,128)S(1)}, u32[]{:S(2)}, u32[]{:S(2)}) collective-permute-start(f32[256,512]{1,0:T(8,128)S(1)} %collective-permute-done.1), channel_id=1, source_target_pairs={{128,0},{256,128},{384,256},{0,384},{129,1},{257,129},{385,257},{1... | collective-permute-start | bytes 1572872 | tf_op jit(solution)/shard_map/ppermute | solution.py:24
  51.1 1.9 %collective-permute-start.7 = (f32[256,512]{1,0:T(8,128)S(1)}, f32[256,512]{1,0:T(8,128)S(1)}, u32[]{:S(2)}, u32[]{:S(2)}) collective-permute-start(f32[256,512]{1,0:T(8,128)S(1)} %collective-permute-done.1), channel_id=1, source_target_pairs={{384,0},{0,128},{128,256},{256,384},{385,1},{1,129},{129,257},{257... | collective-permute-start | bytes 1572872 | tf_op jit(solution)/shard_map/ppermute | solution.py:24
  53.0 1.0 fusion.2
  54.0 0.0 collective-permute-done.4
  54.0 0.0 collective-permute-done.5
  54.0 0.1 fusion.23
  54.1 1.0 fusion.3
  55.1 7.2 %collective-permute-done.6 = f32[256,512]{1,0:T(8,128)S(1)} collective-permute-done((f32[256,512]{1,0:T(8,128)S(1)}, f32[256,512]{1,0:T(8,128)S(1)}, u32[]{:S(2)}, u32[]{:S(2)}) %collective-permute-start.6) | collective-permute-done | bytes 524320 | tf_op jit(solution)/shard_map/ppermute | solution.py:24
  62.3 5.2 %collective-permute-start.8 = (f32[128,512]{1,0:T(8,128)S(1)}, f32[128,512]{1,0:T(8,128)S(1)}, u32[]{:S(2)}, u32[]{:S(2)}) collective-permute-start(f32[128,512]{1,0:T(8,128)S(1)} %slice.42), channel_id=1, source_target_pairs={{128,0},{256,128},{384,256},{0,384},{129,1},{257,129},{385,257},{1... | collective-permute-start | bytes 786440 | tf_op jit(solution)/shard_map/ppermute | solution.py:24
  67.5 0.0 collective-permute-done.7
  67.6 1.9 %collective-permute-start.9 = (f32[128,512]{1,0:T(8,128)S(1)}, f32[128,512]{1,0:T(8,128)S(1)}, u32[]{:S(2)}, u32[]{:S(2)}) collective-permute-start(f32[128,512]{1,0:T(8,128)S(1)} %slice.43), channel_id=1, source_target_pairs={{384,0},{0,128},{128,256},{256,384},{385,1},{1,129},{129,257},{257... | collective-permute-start | bytes 786440 | tf_op jit(solution)/shard_map/ppermute | solution.py:24
  69.5 0.1 fusion.24
  69.6 0.9 fusion.4
  70.5 0.1 fusion.25
  70.6 1.0 fusion.5
  71.5 0.3 collective-permute-done.8
  71.9 5.3 %collective-permute-done.9 = f32[128,512]{1,0:T(8,128)S(1)} collective-permute-done((f32[128,512]{1,0:T(8,128)S(1)}, f32[128,512]{1,0:T(8,128)S(1)}, u32[]{:S(2)}, u32[]{:S(2)}) %collective-permute-start.9) | collective-permute-done | bytes 262176 | tf_op jit(solution)/shard_map/ppermute | solution.py:24
  77.3 0.1 fusion.26
  77.3 0.9 fusion.6
  78.3 0.0 all-to-all-done
  78.3 0.1 copy.8
  78.4 0.1 constant_dynamic-slice_fusion
  78.4 0.1 reshape.57
  78.6 6.1 %fusion.13 = f32[192,2048]{1,0:T(8,128)} fusion(bf16[2048,1536]{1,0:T(8,128)(2,1)} %bitcast.13, bf16[192,512]{1,0:T(8,128)(2,1)S(1)} %get-tuple-element.28, bf16[192,512]{1,0:T(8,128)(2,1)S(1)} %get-tuple-element.27), kind=kOutput, calls=%fused_computation.37 | convolution fusion | flops 1209729024 | bytes 8257536 | tf_op jit(solution)/shard_map/dot_general | solution.py:17
  84.7 1.9 %collective-permute-start.10 = (f32[192,2048]{1,0:T(8,128)}, f32[192,2048]{1,0:T(8,128)S(1)}, u32[]{:S(2)}, u32[]{:S(2)}) collective-permute-start(f32[192,2048]{1,0:T(8,128)} %fusion.13), channel_id=1, source_target_pairs={{1,0},{0,1},{3,2},{2,3},{5,4},{4,5},{7,6},{6,7},{9,8},{8,9},{11,10... | collective-permute-start | bytes 4718600 | tf_op jit(solution)/shard_map/ppermute | solution.py:24
  86.6 0.1 reshape.55
  86.7 5.0 %fusion.7 = f32[192,2048]{1,0:T(8,128)S(1)} fusion(bf16[2048,1536]{1,0:T(8,128)(2,1)} %bitcast.13, bf16[192,512]{1,0:T(8,128)(2,1)S(1)} %get-tuple-element.30, bf16[192,512]{1,0:T(8,128)(2,1)S(1)} %get-tuple-element.29), kind=kOutput, calls=%fused_computation.31 | convolution fusion | flops 1209729024 | bytes 8257536 | tf_op jit(solution)/shard_map/dot_general | solution.py:17
  91.7 0.0 collective-permute-done.10
  91.7 0.2 add.107
  91.9 25.8 %all_to_all.15 = f32[4,48,2048]{2,1,0:T(8,128)S(1)} all-to-all(f32[4,48,2048]{2,1,0:T(8,128)S(1)} %bitcast.60), channel_id=1, replica_groups=mesh['x'=4,'s'=4,'p'=2,'zh'=2,'y'=4,'c'=2] {'y'}, dimensions={0} | all-to-all | bytes 3145728 | tf_op jit(solution)/shard_map/all_to_all | solution.py:78
  117.8 0.1 fusion.29
  117.9 0.1 copy.14
  118.0 0.1 copy.9
  118.2 40.2 %all_to_all.16 = f32[16,24,256]{2,1,0:T(8,128)S(1)} all-to-all(f32[16,24,256]{2,1,0:T(8,128)S(1)} %bitcast.68), channel_id=1, replica_groups=mesh['x'=4,'s'=4,'p'=2,'zh'=2,'y'=4,'c'=2] {'x','p','zh'}, dimensions={0} | all-to-all | bytes 786432 | tf_op jit(solution)/shard_map/all_to_all | solution.py:82
  158.4 0.1 copy.10
  158.5 0.2 reshape.60
  158.7 0.2 slice_add_fusion.2
  158.9 0.1 copy.18
  159.0 0.1 copy.11
  159.1 0.7 reshape.61
  (11 shorter events, 0.3 us)
Async XLA Ops:
  0.0 15.9 %collective-permute-start = (f32[6,4,2048]{2,1,0:T(4,128)}, f32[6,4,2048]{2,1,0:T(4,128)S(1)}, u32[]{:S(2)}, u32[]{:S(2)}) collective-permute-start(f32[6,4,2048]{2,1,0:T(4,128)} %param.2), channel_id=1, source_target_pairs={{0,0},{2,128},{4,256},{6,384},{128,2},{130,130},{132,258},{134,386... | collective-permute-start | bytes 589832 | tf_op jit(solution)/shard_map/ppermute | solution.py:44
  2.7 33.1 %collective-permute-start.2 = (f32[256,512]{1,0:T(8,128)S(1)}, f32[256,512]{1,0:T(8,128)S(1)}, u32[]{:S(2)}, u32[]{:S(2)}) collective-permute-start(f32[256,512]{1,0:T(8,128)S(1)} %bitcast.63), channel_id=1, source_target_pairs={{128,0},{256,128},{384,256},{0,384},{129,1},{257,129},{385,257},{1... | collective-permute-start | bytes 1572872 | tf_op jit(solution)/shard_map/ppermute | solution.py:24
  10.6 28.0 %collective-permute-start.3 = (f32[256,512]{1,0:T(8,128)S(1)}, f32[256,512]{1,0:T(8,128)S(1)}, u32[]{:S(2)}, u32[]{:S(2)}) collective-permute-start(f32[256,512]{1,0:T(8,128)S(1)} %bitcast.64), channel_id=1, source_target_pairs={{384,0},{0,128},{128,256},{256,384},{385,1},{1,129},{129,257},{257... | collective-permute-start | bytes 1572872 | tf_op jit(solution)/shard_map/ppermute | solution.py:24
  12.5 29.2 %collective-permute-start.1 = (f32[256,512]{1,0:T(8,128)S(1)}, f32[256,512]{1,0:T(8,128)S(1)}, u32[]{:S(2)}, u32[]{:S(2)}) collective-permute-start(f32[256,512]{1,0:T(8,128)S(1)} %bitcast.65), channel_id=1, source_target_pairs={{16,0},{0,16},{17,1},{1,17},{18,2},{2,18},{19,3},{3,19},{20,4},{4,... | collective-permute-start | bytes 1572872 | tf_op jit(solution)/shard_map/ppermute | solution.py:24
  17.1 61.2 %all-to-all-start = ((f32[64,24,128]{2,1,0:T(8,128)}), f32[64,24,128]{2,1,0:T(8,128)S(1)}, u32[]{:S(2)}, u32[]{:S(2)}) async-start(f32[64,24,128]{2,1,0:T(8,128)} %bitcast.2), calls=%async_computation | async-start | bytes 1572864 | tf_op jit(solution)/shard_map/all_to_all | solution.py:51
  35.8 18.1 %collective-permute-start.4 = (f32[128,512]{1,0:T(8,128)S(1)}, f32[128,512]{1,0:T(8,128)S(1)}, u32[]{:S(2)}, u32[]{:S(2)}) collective-permute-start(f32[128,512]{1,0:T(8,128)S(1)} %slice.40), channel_id=1, source_target_pairs={{128,0},{256,128},{384,256},{0,384},{129,1},{257,129},{385,257},{1... | collective-permute-start | bytes 786440 | tf_op jit(solution)/shard_map/ppermute | solution.py:24
  38.6 15.4 %collective-permute-start.5 = (f32[128,512]{1,0:T(8,128)S(1)}, f32[128,512]{1,0:T(8,128)S(1)}, u32[]{:S(2)}, u32[]{:S(2)}) collective-permute-start(f32[128,512]{1,0:T(8,128)S(1)} %slice.41), channel_id=1, source_target_pairs={{384,0},{0,128},{128,256},{256,384},{385,1},{1,129},{129,257},{257... | collective-permute-start | bytes 786440 | tf_op jit(solution)/shard_map/ppermute | solution.py:24
  47.0 15.2 %collective-permute-start.6 = (f32[256,512]{1,0:T(8,128)S(1)}, f32[256,512]{1,0:T(8,128)S(1)}, u32[]{:S(2)}, u32[]{:S(2)}) collective-permute-start(f32[256,512]{1,0:T(8,128)S(1)} %collective-permute-done.1), channel_id=1, source_target_pairs={{128,0},{256,128},{384,256},{0,384},{129,1},{257,129},{385,257},{1... | collective-permute-start | bytes 1572872 | tf_op jit(solution)/shard_map/ppermute | solution.py:24
  51.1 16.5 %collective-permute-start.7 = (f32[256,512]{1,0:T(8,128)S(1)}, f32[256,512]{1,0:T(8,128)S(1)}, u32[]{:S(2)}, u32[]{:S(2)}) collective-permute-start(f32[256,512]{1,0:T(8,128)S(1)} %collective-permute-done.1), channel_id=1, source_target_pairs={{384,0},{0,128},{128,256},{256,384},{385,1},{1,129},{129,257},{257... | collective-permute-start | bytes 1572872 | tf_op jit(solution)/shard_map/ppermute | solution.py:24
  62.3 9.6 %collective-permute-start.8 = (f32[128,512]{1,0:T(8,128)S(1)}, f32[128,512]{1,0:T(8,128)S(1)}, u32[]{:S(2)}, u32[]{:S(2)}) collective-permute-start(f32[128,512]{1,0:T(8,128)S(1)} %slice.42), channel_id=1, source_target_pairs={{128,0},{256,128},{384,256},{0,384},{129,1},{257,129},{385,257},{1... | collective-permute-start | bytes 786440 | tf_op jit(solution)/shard_map/ppermute | solution.py:24
  67.6 9.7 %collective-permute-start.9 = (f32[128,512]{1,0:T(8,128)S(1)}, f32[128,512]{1,0:T(8,128)S(1)}, u32[]{:S(2)}, u32[]{:S(2)}) collective-permute-start(f32[128,512]{1,0:T(8,128)S(1)} %slice.43), channel_id=1, source_target_pairs={{384,0},{0,128},{128,256},{256,384},{385,1},{1,129},{129,257},{257... | collective-permute-start | bytes 786440 | tf_op jit(solution)/shard_map/ppermute | solution.py:24
  84.7 7.0 %collective-permute-start.10 = (f32[192,2048]{1,0:T(8,128)}, f32[192,2048]{1,0:T(8,128)S(1)}, u32[]{:S(2)}, u32[]{:S(2)}) collective-permute-start(f32[192,2048]{1,0:T(8,128)} %fusion.13), channel_id=1, source_target_pairs={{1,0},{0,1},{3,2},{2,3},{5,4},{4,5},{7,6},{6,7},{9,8},{8,9},{11,10... | collective-permute-start | bytes 4718600 | tf_op jit(solution)/shard_map/ppermute | solution.py:24
